TPU v7x, 256 devices: a whole 4x4x8 slice. The times are simulated.
256 devices in a mesh: chain: 8 (over y, core), cols: 32 (over x, z).
Axes of the slice: x: 4, y: 4, z: 8, core: 2. Of those that a mesh axis runs over, the one named last changes fastest.
Arguments:
- factor: float32 [4608, 4608], P(('chain', 'cols')), may hold values from -2 to 2, as said below
- right_side: float32 [4608, 16384], P('chain', 'cols'), may hold values from -6 to 6
- occ_order: int32 [64], replicated, may hold values from 0 to 63, each once
- cabs_order: int32 [256], replicated, may hold values from 0 to 255, each once
Outputs:
- fitted: float32 [64, 256, 4608], P('cols', None, 'chain')
Inputs may be any that keep to these rules, and one draw needn't show every extreme that they name: factor is lower triangular: zero above the diagonal, its diagonal between 1 and 2.
All inputs are finite; a program needn't handle non-finite values.
Results may differ from a plain program's by a relative error of at most 0.00017.
Values sent between devices are 32-bit elements; how exact they have to be, the bound alone decides.
No kernel may reach another device: no remote copies, remote signals or barrier semaphores. Data moves between devices by JAX's collectives and lax.ppermute only.
A program may use at most 128 MiB of HBM per device.

v0:
```python
import functools
import jax
import jax.numpy as jnp
from jax import lax
from jax.experimental import pallas as pl
from jax.experimental.pallas import tpu as pltpu
from jax.sharding import Mesh, PartitionSpec as P

HI = lax.Precision.HIGHEST
LANES = 128


def full_dot(left, right):
    return jnp.dot(left, right, precision=HI, preferred_element_type=jnp.float32)


def halves(value):
    high = value.astype(jnp.bfloat16)
    return high, (value - high.astype(jnp.float32)).astype(jnp.bfloat16)


def split_right(value):
    high, low = halves(value)
    return jnp.concatenate([high, low], axis=1), high


def three_dot(left, right):
    lh, ll = left
    both, rh = right
    dot = functools.partial(jnp.dot, preferred_element_type=jnp.float32)
    wide = dot(lh, both)
    return wide[:, :LANES] + (wide[:, LANES:] + dot(ll, rh))


def invert_kernel(rows, groups, pieces, tiles, x_ref, own_ref, left_ref, far0_ref, far1_ref, right_ref, o_ref, a_ref, m_ref):
    per = rows // (groups * pieces)
    wide = 640
    blocks = wide // LANES
    x = x_ref[0]
    half = pieces // 2
    for ref, back, first, count in (
        (own_ref, 0, 0, pieces),
        (left_ref, 1, 0, pieces),
        (far0_ref, 2, 0, half),
        (far1_ref, 2, half, half),
        (right_ref, 3, 0, pieces),
    ):
        base = (lax.rem(x + groups - back, groups) * pieces + first) * per
        for tile in range(tiles):
            for row in range(per):
                a_ref[tile, pl.ds(base + row, count, stride=per), :] = ref[
                    pl.ds(row * tiles + tile, count, stride=per * tiles), :
                ]
    extra = wide - rows
    r0 = lax.broadcasted_iota(jnp.int32, (extra, LANES), 0)
    c0 = lax.broadcasted_iota(jnp.int32, (extra, LANES), 1)
    for tile in range(blocks - 1):
        a_ref[tile, rows:wide, :] = jnp.zeros((extra, LANES), jnp.float32)
    a_ref[blocks - 1, rows:wide, :] = jnp.where(c0 == r0 + (LANES - extra), 1.0, 0.0)
    ri = lax.broadcasted_iota(jnp.int32, (LANES, LANES), 0)
    ci = lax.broadcasted_iota(jnp.int32, (LANES, LANES), 1)

    def block(i, j):
        return a_ref[j, i * LANES : (i + 1) * LANES, :]

    for i in range(blocks):
        m_ref[i] = jnp.where(ri == ci, 1.0 / jnp.where(ri == ci, block(i, i), 1.0), 0.0)

    def double(level, carry):
        rb, cb = ri >> level, ci >> level
        take = (rb >> 1 == cb >> 1) & (rb == cb + 1)
        mids = [full_dot(jnp.where(take, block(i, i), 0.0), m_ref[i]) for i in range(blocks)]
        news = [m_ref[i] - full_dot(m_ref[i], mids[i]) for i in range(blocks)]
        for i in range(blocks):
            m_ref[i] = news[i]
        return carry

    lax.fori_loop(0, 7, double, 0)
    inv = [m_ref[i] for i in range(blocks)]
    for i in range(blocks):
        for j in range(blocks):
            last = min((i + 1) * LANES, rows)
            if j > i:
                o_ref[i * LANES : last, j * LANES : (j + 1) * LANES] = jnp.zeros((last - i * LANES, LANES), jnp.float32)
    done = [[None] * blocks for _ in range(blocks)]
    for i in range(blocks):
        done[i][i] = inv[i]
        last = min((i + 1) * LANES, rows)
        for j in range(i):
            total = full_dot(block(i, j), done[j][j])
            for k in range(j + 1, i):
                total = total + full_dot(block(i, k), done[k][j])
            done[i][j] = -full_dot(inv[i], total)
        for j in range(i + 1):
            o_ref[i * LANES : last, j * LANES : (j + 1) * LANES] = done[i][j][: last - i * LANES]
    for tile in range(blocks, tiles):
        o_ref[:, tile * LANES : (tile + 1) * LANES] = a_ref[tile, :rows, :]


def order_kernel(rows, pieces, pad_rows, first, tiles, whole_ref, o_ref, s_ref):
    per = rows // pieces
    for tile in range(tiles):

        def move(row, carry):
            s_ref[pl.ds(row, pieces, stride=per), :] = whole_ref[
                pl.ds(first + row * tiles + tile, pieces, stride=pad_rows), :
            ]
            return carry

        lax.fori_loop(0, per, move, 0, unroll=6)
        o_ref[:, tile * LANES : (tile + 1) * LANES] = s_ref[...]


def pack_kernel(core_ref, own_ref, other_ref, o_ref):
    core = core_ref[0]
    rows = own_ref.shape[0]
    for start in range(0, rows, 192):
        here = slice(start, start + 192)
        high, low = halves(own_ref[here, :])
        o_ref[core, 0, here, :] = high
        o_ref[core, 1, here, :] = low
        high, low = halves(other_ref[here, :])
        o_ref[1 - core, 0, here, :] = high
        o_ref[1 - core, 1, here, :] = low


def solve(state, e_ref, x_ref, rows):
    wide = 640
    step = rows // 3

    def put_first(index, value):
        x_ref[pl.ds(pl.multiple_of(index * step, step), step), :] = value

    def put_second(index, value):
        x_ref[pl.ds(pl.multiple_of(rows + index * step, step), step), :] = value

    def take(index, value):
        here = pl.ds(pl.multiple_of(rows + index * step, step), step)
        state[here, :] = state[here, :] - value

    def product(left, right, put):
        def part(index, carry):
            here = pl.ds(pl.multiple_of(index * step, step), step)
            total = None
            for (which, start, size), operand in zip(left, right):
                pair = e_ref[which, 0, here, start : start + size], e_ref[which, 1, here, start : start + size]
                term = three_dot(pair, operand)
                total = term if total is None else total + term
            put(index, total)
            return carry

        lax.fori_loop(0, 3, part, 0)

    half, link = rows // 2, e_ref.shape[3] - wide
    product([(0, 0, wide)], [split_right(state[0:wide, :])], put_first)
    tail = jnp.concatenate([x_ref[half:rows, :], jnp.zeros((link - half, LANES), jnp.float32)], axis=0)
    head = x_ref[0:link, :]
    product([(1, wide, link), (0, wide, link)], [split_right(head), split_right(tail)], take)
    product([(1, 0, wide)], [split_right(state[rows : rows + wide, :])], put_second)


def place_kernel(got_ref, place_ref, *outs):
    cores, _, rows = got_ref.shape
    for core in range(cores):
        for index, out in enumerate(outs):
            out[core * rows : (core + 1) * rows, :] = lax.dot_general(
                got_ref[core],
                place_ref[:, index * LANES : (index + 1) * LANES],
                (((0,), (0,)), ((), ())),
                precision=HI,
                preferred_element_type=jnp.float32,
            )


def load_state(state, r_ref, span):
    state[0:span, :] = r_ref[...]
    state[span:, :] = jnp.zeros((state.shape[0] - span, LANES), jnp.float32)


def subtract(state, l_ref, x_ref):
    x = split_right(x_ref[...])
    cores, _, rows, _ = l_ref.shape
    step = rows // 2

    def part(index, carry):
        core, piece = index // 2, index % 2
        here = pl.ds(pl.multiple_of(piece * step, step), step)
        there = pl.ds(pl.multiple_of(index * step, step), step)
        state[there, :] = state[there, :] - three_dot((l_ref[core, 0, here, :], l_ref[core, 1, here, :]), x)
        return carry

    lax.fori_loop(0, 2 * cores, part, 0)


def pick(plane, first, first_ref, second, second_ref, to_ref):
    @pl.when(plane == first)
    def _():
        to_ref[...] = first_ref[...]

    @pl.when(plane == second)
    def _():
        to_ref[...] = second_ref[...]


def stage_kernel(rows, number, plane_ref, *refs):
    plane = plane_ref[0]
    span = 2 * rows
    e_ref, refs = refs[0], refs[1:]
    a_ref, refs = (refs[0], refs[1:]) if number in (1, 2) else (None, refs)
    b_ref, refs = (refs[0], refs[1:]) if number >= 2 else (None, refs)
    r_ref, refs = refs[0], refs[1:]
    arrived = refs[: (0, 2, 3, 2)[number]]
    outs = refs[len(arrived) : len(arrived) + (2 if number == 1 else 1)]
    state, seen = refs[len(arrived) + len(outs) :]
    x_ref = outs[-1]
    other = {1: 3, 2: 0}.get(number)
    works = plane == number if other is None else (plane == number) | (plane == other)

    @pl.when(works)
    def _():
        load_state(state, r_ref, span)
        if number in (1, 2):
            pick(plane, number, arrived[0], other, arrived[1], seen)
            if number == 2:

                @pl.when(plane == 0)
                def _():
                    state[...] = jnp.zeros_like(state)

            subtract(state, a_ref, seen)
        if number == 3:
            state[0:span, :] = state[0:span, :] + arrived[0][...]

    if number == 1:
        outs[0][...] = jnp.where(plane == 3, state[0:span, :], r_ref[...])

    @pl.when(plane == number)
    def _():
        if number >= 2:
            subtract(state, b_ref, arrived[-1])
        solve(state, e_ref, x_ref, rows)

    if number == 2:

        @pl.when(plane == 0)
        def _():
            x_ref[...] = state[0:span, :]

        @pl.when((plane == 1) | (plane == 3))
        def _():
            x_ref[...] = jnp.zeros_like(x_ref)
    else:

        @pl.when(plane != number)
        def _():
            x_ref[...] = jnp.zeros_like(x_ref)


def per_device(factor, right_side, occ_order, cabs_order):
    planes, cores = lax.axis_size("y"), lax.axis_size("core")
    plane, core = lax.axis_index("y"), lax.axis_index("core")
    pieces = lax.axis_size("x") * lax.axis_size("z")
    per, aux = factor.shape
    rows = per * pieces
    span = cores * rows
    occ_total, cabs_total = occ_order.shape[0], cabs_order.shape[0]
    cabs_local = right_side.shape[1] // occ_total
    cheap = pl.CostEstimate(flops=1000, bytes_accessed=1000, transcendentals=0)
    small = pltpu.CompilerParams(vmem_limit_bytes=8 * 1024 * 1024)
    large = pltpu.CompilerParams(vmem_limit_bytes=24 * 1024 * 1024)

    slots = occ_order.reshape(pieces, cores).T.reshape(occ_total)
    pick = (jnp.arange(cabs_local, dtype=jnp.int32)[None, :] * occ_total + slots[:, None]).reshape(-1, 1)
    spread = (pick == jnp.arange(right_side.shape[1], dtype=jnp.int32)[None, :]).astype(jnp.float32)
    sent = lax.dot_general(spread, right_side, (((1,), (1,)), ((), ())), precision=HI, preferred_element_type=jnp.float32)
    sent = sent.reshape(occ_total, cabs_local, rows)

    swap = [(0, 1), (1, 0)]
    x_arg = lax.axis_index("x").reshape(1).astype(jnp.int32)
    smem = pl.BlockSpec(memory_space=pltpu.SMEM)
    here = pl.BlockSpec(memory_space=pltpu.VMEM)
    zs, xs = lax.axis_size("z"), lax.axis_size("x")
    diag = lax.dynamic_slice_in_dim(factor, plane * span, span, 1)
    low, high = diag[:, :rows], diag[:, rows:]
    half = rows // 2
    gap, short = jnp.zeros((per, 640 - rows), jnp.float32), jnp.zeros((per, 384 - half), jnp.float32)
    lent = lax.ppermute(low[:, half:], "core", [(1, 0)])
    diag = jnp.where(
        core == 0,
        jnp.concatenate([low, gap, lent, short], axis=1),
        jnp.concatenate([high, gap, low[:, :half], short], axis=1),
    )
    tiles = diag.shape[1] // LANES

    def spread(part):
        copies = jnp.broadcast_to(part[None], (zs, *part.shape))
        return lax.all_to_all(copies, "z", 0, 0, tiled=True).reshape(zs * part.shape[0], LANES)

    got = lax.all_to_all(sent, ("core", "x", "z"), 0, 0, tiled=True)
    marker = lax.ppermute(sent[:1, :, :LANES], "core", swap)
    piece, marker = lax.optimization_barrier((diag.reshape(per * tiles, LANES), marker))
    x_arg = x_arg + (marker[0, 0, :1] != marker[0, 0, :1]).astype(jnp.int32)
    near = spread(piece)
    ahead = [(i, (i + 1) % xs) for i in range(xs)]
    behind = [(i, (i - 1) % xs) for i in range(xs)]

    def flat(block):
        return jnp.pad(block.reshape(per * ltiles, LANES), ((0, lpad - per * ltiles), (0, 0)))

    ltiles = span // LANES
    lpad = (per * ltiles + 7) // 8 * 8
    moved = lax.ppermute(factor[:, span : 2 * span], "y", [(3, 0)])
    flat_a = flat(jnp.where(plane == 0, moved, factor[:, :span]))
    flat_b = flat(lax.dynamic_slice_in_dim(factor, jnp.maximum(plane - 1, 0) * span, span, 1))
    left, right = lax.ppermute(near, "x", ahead), lax.ppermute(near, "x", behind)
    whole = lax.all_gather(jnp.concatenate([flat_a, flat_b]), ("x", "z"), axis=0, tiled=True)

    def far(left, right):
        middle = left.shape[0] // 2
        return lax.ppermute(left[:middle], "x", ahead), lax.ppermute(right[middle:], "x", behind)

    far0, far1 = far(left, right)
    far0, far1, got = lax.optimization_barrier((far0, far1, got))
    got = got.reshape(cores, cabs_total, rows)
    place = (jnp.arange(cabs_total, dtype=jnp.int32)[:, None] == cabs_order[None, :]).astype(jnp.float32)
    states = list(pl.pallas_call(
        place_kernel,
        out_shape=(jax.ShapeDtypeStruct((span, LANES), jnp.float32),) * (cabs_total // LANES),
        in_specs=[here, here],
        out_specs=(here,) * (cabs_total // LANES),
        compiler_params=small,
        cost_estimate=cheap,
        name="place",
    )(got, place))
    mine = pl.pallas_call(
        functools.partial(invert_kernel, rows, xs, zs, tiles),
        out_shape=jax.ShapeDtypeStruct((rows, tiles * LANES), jnp.float32),
        in_specs=[smem] + [here] * 5,
        out_specs=here,
        scratch_shapes=[pltpu.VMEM((tiles, 640, LANES), jnp.float32), pltpu.VMEM((5, LANES, LANES), jnp.float32)],
        compiler_params=pltpu.CompilerParams(vmem_limit_bytes=12 * 1024 * 1024),
        cost_estimate=cheap,
        name="invert",
    )(x_arg, near, left, far0, far1, right)
    theirs = lax.ppermute(mine, "core", swap)
    core_arg = core.reshape(1).astype(jnp.int32)
    plane_arg = plane.reshape(1).astype(jnp.int32)
    inverse = pl.pallas_call(
        pack_kernel,
        out_shape=jax.ShapeDtypeStruct((cores, 2, rows, tiles * LANES), jnp.bfloat16),
        in_specs=[smem, here, here],
        out_specs=here,
        compiler_params=small,
        cost_estimate=cheap,
        name="pack",
    )(core_arg, mine, theirs)

    def after(value, tokens):
        value, token = lax.optimization_barrier((value, sum(token[0, :1] for token in tokens)))
        return value, (token != token).astype(jnp.int32)

    def paired(own, zero):
        other = lax.ppermute(own, "core", swap)
        return pl.pallas_call(
            pack_kernel,
            out_shape=jax.ShapeDtypeStruct((cores, 2, *own.shape), jnp.bfloat16),
            in_specs=[smem, here, here],
            out_specs=here,
            compiler_params=small,
            cost_estimate=pl.CostEstimate(flops=1_000_000, bytes_accessed=8_000_000, transcendentals=0),
            name="pack",
        )(core_arg + zero, own, other)

    def ordered(which, whole, zero):
        own = pl.pallas_call(
            functools.partial(order_kernel, rows, pieces, 2 * lpad, which * lpad, ltiles),
            out_shape=jax.ShapeDtypeStruct((rows, span), jnp.float32),
            in_specs=[here],
            out_specs=here,
            scratch_shapes=[pltpu.VMEM((rows, LANES), jnp.float32)],
            compiler_params=small,
            cost_estimate=pl.CostEstimate(flops=1_000_000, bytes_accessed=8_000_000, transcendentals=0),
            name="order",
        )(whole)
        return paired(own, zero)

    block = jax.ShapeDtypeStruct((span, LANES), jnp.float32)

    def stage(number, *args):
        outs = 2 if number == 1 else 1
        return pl.pallas_call(
            functools.partial(stage_kernel, rows, number),
            out_shape=(block,) * outs,
            in_specs=[smem] + [here] * len(args),
            out_specs=(here,) * outs,
            scratch_shapes=[pltpu.VMEM((span + 64, LANES), jnp.float32), pltpu.VMEM((span, LANES), jnp.float32)],
            compiler_params=small,
            cost_estimate=pl.CostEstimate(flops=30_000_000_000, bytes_accessed=4_000_000, transcendentals=0),
            name=f"stage{number}",
        )(plane_arg, *args)

    def send(value, pairs):
        return lax.ppermute(value, "y", pairs)

    x0s, chunks = [], []
    for state in states:
        x0s += stage(0, inverse, state)
    firsts = [(send(x0, [(0, 1)]), send(x0, [(0, 3)])) for x0 in x0s]
    whole, zero = after(whole, [*firsts[0], x0s[-1]])
    a_mat = ordered(0, whole, zero)
    x1s, nexts = [], []
    for index, (state, (to1, to3)) in enumerate(zip(list(states), firsts)):
        to2 = send(to3, [(3, 2)])
        states[index], x1 = stage(1, inverse, a_mat, state, to1, to3)
        near_x, to0 = send(x1, [(1, 2)]), send(x1, [(1, 0)])
        x1s.append((x1, to2))
        nexts.append((near_x, to0))
    _, zero = after(core_arg, [x1 for x1, _ in x1s])
    b_mat = ordered(1, whole, zero)
    for state, x0, (x1, to2), (near_x, to0) in zip(states, x0s, x1s, nexts):
        (x2,) = stage(2, inverse, a_mat, b_mat, state, to2, to0, near_x)
        part = send(x2, [(0, 3)])
        near_x = send(x2, [(2, 3)])
        (x3,) = stage(3, inverse, b_mat, state, part, near_x)
        chunks.append(jnp.where(plane == 0, x0, jnp.where(plane == 1, x1, jnp.where(plane == 2, x2, x3))))
    solved = jnp.concatenate([x.T for x in chunks], axis=0)
    keep = jnp.where(core == 0, solved[:, :rows], solved[:, rows:])
    give = jnp.where(core == 0, solved[:, rows:], solved[:, :rows])
    came = lax.ppermute(give, "core", [(0, 1), (1, 0)])
    return jnp.where(core == 0, jnp.stack([keep, came]), jnp.stack([came, keep]))


def solution(mesh):
    grid = Mesh(mesh.devices.reshape(4, 2, 4, 8), ("y", "core", "x", "z"))
    in_specs = (P(("y", "core", "x", "z"), None), P(("y", "core"), ("x", "z")), P(), P())
    out_specs = P(("x", "z"), None, ("y", "core"))
    return jax.shard_map(per_device, mesh=grid, in_specs=in_specs, out_specs=out_specs, check_vma=False)
```

profile of v0, /device:TPU:31, one launch (start us, length us, event | category | flops | bytes accessed | tf_op | source)
XLA Modules:
  0.0 232.9 jit_solution(12858154626716066886)
XLA Ops:
  7.5 2.6 %collective-permute-start = (f32[18,288]{1,0:T(8,128)S(1)}, f32[18,288]{1,0:T(8,128)S(1)}, u32[]{:S(2)}, u32[]{:S(2)}) collective-permute-start(f32[18,288]{1,0:T(8,128)S(1)} %get-tuple-element.40), channel_id=1, source_target_pairs={{32,0},{33,1},{34,2},{35,3},{36,4},{37,5},{38,6},{39,7},{40,8},{41... | collective-permute-start | bytes 62216 | tf_op jit(solution)/shard_map/ppermute | solution.py:287
  14.9 8.2 %all-to-all-start = ((f32[8,144,128]{2,1,0:T(8,128)}), f32[8,144,128]{2,1,0:T(8,128)S(1)}, u32[]{:S(2)}, u32[]{:S(2)}) async-start(f32[8,144,128]{2,1,0:T(8,128)} %broadcast_in_dim.8), calls=%async_computation | async-start | bytes 1179648 | tf_op jit(solution)/shard_map/all_to_all | solution.py:297
  23.8 2.5 %collective-permute-start.7 = (f32[18,1152]{1,0:T(8,128)}, f32[18,1152]{1,0:T(8,128)}, u32[]{:S(2)}, u32[]{:S(2)}) collective-permute-start(f32[18,1152]{1,0:T(8,128)} %slice.64), channel_id=1, source_target_pairs={{192,0},{193,1},{194,2},{195,3},{196,4},{197,5},{198,6},{199,7},{2... | collective-permute-start | bytes 248840 | tf_op jit(solution)/shard_map/ppermute | solution.py:312
  31.2 11.4 %all-to-all-done = f32[8,144,128]{2,1,0:T(8,128)S(1)} async-done(((f32[8,144,128]{2,1,0:T(8,128)}), f32[8,144,128]{2,1,0:T(8,128)S(1)}, u32[]{:S(2)}, u32[]{:S(2)}) %all-to-all-start) | async-done | bytes 589856 | tf_op jit(solution)/shard_map/all_to_all | solution.py:297
  42.5 5.7 %all-to-all-start.1 = ((f32[64,8,576]{2,1,0:T(8,128)}), f32[64,8,576]{2,1,0:T(8,128)S(1)}, u32[]{:S(2)}, u32[]{:S(2)}) async-start(f32[64,8,576]{2,1,0:T(8,128)} %copy-done.16), calls=%async_computation.1 | async-start | bytes 2621440 | tf_op jit(solution)/shard_map/all_to_all | solution.py:299
  49.8 25.5 %collective-permute-done.2.left_ref = f32[1152,128]{1,0:T(8,128)S(1)} collective-permute-done((f32[1152,128]{1,0:T(8,128)S(1)}, f32[1152,128]{1,0:T(8,128)S(1)}, u32[]{:S(2)}, u32[]{:S(2)}) %collective-permute-start.2) | collective-permute-done | bytes 589856 | tf_op jit(solution)/shard_map/ppermute | solution.py:315
  76.1 2.0 collective-permute-start.3
  80.8 6.7 %collective-permute-done.3.far0_ref = f32[576,128]{1,0:T(8,128)S(1)} collective-permute-done((f32[576,128]{1,0:T(8,128)}, f32[576,128]{1,0:T(8,128)S(1)}, u32[]{:S(2)}, u32[]{:S(2)}) %collective-permute-start.3) | collective-permute-done | bytes 294944 | tf_op jit(solution)/shard_map/ppermute | solution.py:320
  87.5 2.8 %collective-permute-done.5.far1_ref = f32[576,128]{1,0:T(8,128)} collective-permute-done((f32[576,128]{1,0:T(8,128)}, f32[576,128]{1,0:T(8,128)}, u32[]{:S(2)}, u32[]{:S(2)}) %collective-permute-start.5) | collective-permute-done | bytes 294944 | tf_op jit(solution)/shard_map/ppermute | solution.py:320
  92.5 10.6 %invert.1.own_ref = f32[576,1024]{1,0:T(8,128)S(1)} custom-call(s32[1]{0:T(128)S(6)} %add.64.x_ref, f32[1152,128]{1,0:T(8,128)S(1)} %bitcast.24, f32[1152,128]{1,0:T(8,128)S(1)} %copy-done.5, f32[576,128]{1,0:T(8,128)S(1)} %collective-permute-done.3.far0_ref, f32[576,128]{1,0:T(8,128)} %collective-permute-done.5.far1_ref, f32[1152,128]{1,0:T(8,128)S(1)} %copy-done.7), custom_call_target="tpu_custom_call" | custom-call | flops 1000 | bytes 1000 | tf_op jit(solution)/shard_map/invert/pallas_call | solution.py:335
  104.5 2.3 %place.1 = (f32[1152,128]{1,0:T(8,128)S(1)}, f32[1152,128]{1,0:T(8,128)S(1)}) custom-call(f32[2,256,576]{2,1,0:T(8,128)S(1)} %bitcast.19, f32[256,256]{1,0:T(8,128)S(1)} %fusion.2.place_ref), custom_call_target="tpu_custom_call" | custom-call | flops 1000 | bytes 1000 | tf_op jit(solution)/shard_map/place/pallas_call | solution.py:326
  113.0 15.7 %collective-permute-done.9.refs_4_ = f32[1152,128]{1,0:T(8,128)S(1)} collective-permute-done((f32[1152,128]{1,0:T(8,128)S(1)}, f32[1152,128]{1,0:T(8,128)S(1)}, u32[]{:S(2)}, u32[]{:S(2)}) %collective-permute-start.9) | collective-permute-done | bytes 589856 | tf_op jit(solution)/shard_map/ppermute | solution.py:403
  131.2 2.6 %copy-done.1 = f32[10752,128]{1,0:T(8,128)S(1)} copy-done((f32[10752,128]{1,0:T(8,128)S(1)}, f32[10752,128]{1,0:T(8,128)}, u32[]{:S(2)}) %copy-start.1) | copy-done | bytes 5505048
  133.8 2.8 %order.2.own_ref = f32[576,1152]{1,0:T(8,128)} custom-call(f32[10752,128]{1,0:T(8,128)S(1)} %copy-done.1), custom_call_target="tpu_custom_call" | custom-call | flops 1000000 | bytes 8000000 | tf_op jit(solution)/shard_map/order/pallas_call | solution.py:375
  140.8 14.7 %collective-permute-done.12.refs_4_ = f32[1152,128]{1,0:T(8,128)S(1)} collective-permute-done((f32[1152,128]{1,0:T(8,128)S(1)}, f32[1152,128]{1,0:T(8,128)S(1)}, u32[]{:S(2)}, u32[]{:S(2)}) %collective-permute-start.12) | collective-permute-done | bytes 589856 | tf_op jit(solution)/shard_map/ppermute | solution.py:403
  156.8 2.6 %copy-done.2 = f32[10752,128]{1,0:T(8,128)S(1)} copy-done((f32[10752,128]{1,0:T(8,128)S(1)}, f32[10752,128]{1,0:T(8,128)}, u32[]{:S(2)}) %copy-start.2) | copy-done | bytes 5505048
  161.4 3.3 %pack.4.refs_1_ = bf16[2,2,576,1152]{3,2,1,0:T(8,128)(2,1)S(1)} custom-call(s32[1]{0:T(128)S(6)} %add.69.core_ref, f32[576,1152]{1,0:T(8,128)} %order.2.own_ref, f32[576,1152]{1,0:T(8,128)} %collective-permute-done.10.other_ref), custom_call_target="tpu_custom_call" | custom-call | flops 1000000 | bytes 8000000 | tf_op jit(solution)/shard_map/pack/pallas_call | solution.py:364
  164.8 2.5 %stage1.2 = (f32[1152,128]{1,0:T(8,128)S(1)}, f32[1152,128]{1,0:T(8,128)S(1)}) custom-call(s32[1]{0:T(128)} %bitcast.plane_ref, bf16[2,2,576,1024]{3,2,1,0:T(8,128)(2,1)S(1)} %bitcast.21, bf16[2,2,576,1152]{3,2,1,0:T(8,128)(2,1)S(1)} %pack.4.refs_1_, f32[1152,128]{1,0:T(8,128)S(1)} %copy-done.13, f32[1152,128]{1,0:T(8,128)S(1)} %copy-done.15, ...), custom_call_target="tpu_custom_call" | custom-call | flops 30000001024 | bytes 4000000 | tf_op jit(solution)/shard_map/stage1/pallas_call | solution.py:391
  168.7 2.7 %stage1.3 = (f32[1152,128]{1,0:T(8,128)S(1)}, f32[1152,128]{1,0:T(8,128)S(1)}) custom-call(s32[1]{0:T(128)} %bitcast.plane_ref, bf16[2,2,576,1024]{3,2,1,0:T(8,128)(2,1)S(1)} %bitcast.21, bf16[2,2,576,1152]{3,2,1,0:T(8,128)(2,1)S(1)} %pack.4.refs_1_, f32[1152,128]{1,0:T(8,128)S(1)} %get-tuple-element.25.refs_1_.refs_2_, ...), custom_call_target="tpu_custom_call" | custom-call | flops 30000001024 | bytes 4000000 | tf_op jit(solution)/shard_map/stage1/pallas_call | solution.py:391
  181.5 14.4 %collective-permute-done.17.refs_3_ = f32[1152,128]{1,0:T(8,128)S(1)} collective-permute-done((f32[1152,128]{1,0:T(8,128)S(1)}, f32[1152,128]{1,0:T(8,128)S(1)}, u32[]{:S(2)}, u32[]{:S(2)}) %collective-permute-start.17) | collective-permute-done | bytes 589856 | tf_op jit(solution)/shard_map/ppermute | solution.py:403
  196.0 6.6 %collective-permute-done.18.refs_4_ = f32[1152,128]{1,0:T(8,128)S(1)} collective-permute-done((f32[1152,128]{1,0:T(8,128)S(1)}, f32[1152,128]{1,0:T(8,128)S(1)}, u32[]{:S(2)}, u32[]{:S(2)}) %collective-permute-start.18) | collective-permute-done | bytes 589856 | tf_op jit(solution)/shard_map/ppermute | solution.py:403
  202.6 5.4 %stage3.2 = f32[1152,128]{1,0:T(8,128)S(1)} custom-call(s32[1]{0:T(128)} %bitcast.plane_ref, bf16[2,2,576,1024]{3,2,1,0:T(8,128)(2,1)S(1)} %bitcast.21, bf16[2,2,576,1152]{3,2,1,0:T(8,128)(2,1)S(1)} %pack.5.refs_2_.refs_1_, f32[1152,128]{1,0:T(8,128)S(1)} %get-tuple-element.31.refs_3_.refs_2_, f32[1152,128]{1,0:T(8,128)S(1)} %collective-permute-done.17.refs_3_, ...), custom_call_target="tpu_custom_call" | custom-call | flops 30000001024 | bytes 4000000 | tf_op jit(solution)/shard_map/stage3/pallas_call | solution.py:391
  209.4 6.6 %collective-permute-done.23.refs_4_ = f32[1152,128]{1,0:T(8,128)S(1)} collective-permute-done((f32[1152,128]{1,0:T(8,128)S(1)}, f32[1152,128]{1,0:T(8,128)S(1)}, u32[]{:S(2)}, u32[]{:S(2)}) %collective-permute-start.23) | collective-permute-done | bytes 589856 | tf_op jit(solution)/shard_map/ppermute | solution.py:403
  216.0 5.4 %stage3.3 = f32[1152,128]{1,0:T(8,128)S(1)} custom-call(s32[1]{0:T(128)} %bitcast.plane_ref, bf16[2,2,576,1024]{3,2,1,0:T(8,128)(2,1)S(1)} %bitcast.21, bf16[2,2,576,1152]{3,2,1,0:T(8,128)(2,1)S(1)} %pack.5.refs_2_.refs_1_, f32[1152,128]{1,0:T(8,128)S(1)} %get-tuple-element.32.refs_3_.refs_2_, f32[1152,128]{1,0:T(8,128)S(1)} %collective-permute-done.22.refs_3_, ...), custom_call_target="tpu_custom_call" | custom-call | flops 30000001024 | bytes 4000000 | tf_op jit(solution)/shard_map/stage3/pallas_call | solution.py:391
  (126 shorter events, 48.9 us)
Async XLA Ops:
  7.5 5.7 %collective-permute-start = (f32[18,288]{1,0:T(8,128)S(1)}, f32[18,288]{1,0:T(8,128)S(1)}, u32[]{:S(2)}, u32[]{:S(2)}) collective-permute-start(f32[18,288]{1,0:T(8,128)S(1)} %get-tuple-element.40), channel_id=1, source_target_pairs={{32,0},{33,1},{34,2},{35,3},{36,4},{37,5},{38,6},{39,7},{40,8},{41... | collective-permute-start | bytes 62216 | tf_op jit(solution)/shard_map/ppermute | solution.py:287
  14.9 27.6 %all-to-all-start = ((f32[8,144,128]{2,1,0:T(8,128)}), f32[8,144,128]{2,1,0:T(8,128)S(1)}, u32[]{:S(2)}, u32[]{:S(2)}) async-start(f32[8,144,128]{2,1,0:T(8,128)} %broadcast_in_dim.8), calls=%async_computation | async-start | bytes 1179648 | tf_op jit(solution)/shard_map/all_to_all | solution.py:297
  23.1 108.1 %all-gather.2.cloned.1.call-start = ((), (), s32[]{:S(2)}) async-start(), calls=%async_computation.2 | async-start | bytes 5677056 | tf_op jit(solution)/shard_map/all_gather | solution.py:316
  23.8 4.1 %collective-permute-start.7 = (f32[18,1152]{1,0:T(8,128)}, f32[18,1152]{1,0:T(8,128)}, u32[]{:S(2)}, u32[]{:S(2)}) collective-permute-start(f32[18,1152]{1,0:T(8,128)} %slice.64), channel_id=1, source_target_pairs={{192,0},{193,1},{194,2},{195,3},{196,4},{197,5},{198,6},{199,7},{2... | collective-permute-start | bytes 248840 | tf_op jit(solution)/shard_map/ppermute | solution.py:312
  42.5 47.7 %all-to-all-start.1 = ((f32[64,8,576]{2,1,0:T(8,128)}), f32[64,8,576]{2,1,0:T(8,128)S(1)}, u32[]{:S(2)}, u32[]{:S(2)}) async-start(f32[64,8,576]{2,1,0:T(8,128)} %copy-done.16), calls=%async_computation.1 | async-start | bytes 2621440 | tf_op jit(solution)/shard_map/all_to_all | solution.py:299
  48.2 27.1 %collective-permute-start.2 = (f32[1152,128]{1,0:T(8,128)S(1)}, f32[1152,128]{1,0:T(8,128)S(1)}, u32[]{:S(2)}, u32[]{:S(2)}) collective-permute-start(f32[1152,128]{1,0:T(8,128)S(1)} %bitcast.22), channel_id=1, source_target_pairs={{0,8},{8,16},{16,24},{24,0},{1,9},{9,17},{17,25},{25,1},{2,10},{10... | collective-permute-start | bytes 1769480 | tf_op jit(solution)/shard_map/ppermute | solution.py:315
  48.3 29.8 %collective-permute-start.4 = (f32[1152,128]{1,0:T(8,128)S(1)}, f32[1152,128]{1,0:T(8,128)S(1)}, u32[]{:S(2)}, u32[]{:S(2)}) collective-permute-start(f32[1152,128]{1,0:T(8,128)S(1)} %bitcast.23), channel_id=1, source_target_pairs={{0,24},{8,0},{16,8},{24,16},{1,25},{9,1},{17,9},{25,17},{2,26},{10... | collective-permute-start | bytes 1769480 | tf_op jit(solution)/shard_map/ppermute | solution.py:315
  76.1 11.4 %collective-permute-start.3 = (f32[576,128]{1,0:T(8,128)}, f32[576,128]{1,0:T(8,128)S(1)}, u32[]{:S(2)}, u32[]{:S(2)}) collective-permute-start(f32[576,128]{1,0:T(8,128)} %slice.74), channel_id=1, source_target_pairs={{0,8},{8,16},{16,24},{24,0},{1,9},{9,17},{17,25},{25,1},{2,10},{10... | collective-permute-start | bytes 884744 | tf_op jit(solution)/shard_map/ppermute | solution.py:320
  79.0 11.3 %collective-permute-start.5 = (f32[576,128]{1,0:T(8,128)}, f32[576,128]{1,0:T(8,128)}, u32[]{:S(2)}, u32[]{:S(2)}) collective-permute-start(f32[576,128]{1,0:T(8,128)} %slice.75), channel_id=1, source_target_pairs={{0,24},{8,0},{16,8},{24,16},{1,25},{9,1},{17,9},{25,17},{2,26},{10... | collective-permute-start | bytes 884744 | tf_op jit(solution)/shard_map/ppermute | solution.py:320
  103.1 5.6 %collective-permute-start.6 = (f32[576,1024]{1,0:T(8,128)S(1)}, f32[576,1024]{1,0:T(8,128)S(1)}, u32[]{:S(2)}, u32[]{:S(2)}) collective-permute-start(f32[576,1024]{1,0:T(8,128)S(1)} %invert.1.own_ref), channel_id=1, source_target_pairs={{0,32},{32,0},{1,33},{33,1},{2,34},{34,2},{3,35},{35,3},{4,36},{36... | collective-permute-start | bytes 7077896 | tf_op jit(solution)/shard_map/ppermute | solution.py:345
  110.2 18.5 %collective-permute-start.9 = (f32[1152,128]{1,0:T(8,128)S(1)}, f32[1152,128]{1,0:T(8,128)S(1)}, u32[]{:S(2)}, u32[]{:S(2)}) collective-permute-start(f32[1152,128]{1,0:T(8,128)S(1)} %stage0.2), channel_id=1, source_target_pairs={{0,192},{1,193},{2,194},{3,195},{4,196},{5,197},{6,198},{7,199},{8... | collective-permute-start | bytes 1769480 | tf_op jit(solution)/shard_map/ppermute | solution.py:403
  136.5 24.9 %collective-permute-start.10 = (f32[576,1152]{1,0:T(8,128)}, f32[576,1152]{1,0:T(8,128)}, u32[]{:S(2)}, u32[]{:S(2)}) collective-permute-start(f32[576,1152]{1,0:T(8,128)} %order.2.own_ref), channel_id=1, source_target_pairs={{0,32},{32,0},{1,33},{33,1},{2,34},{34,2},{3,35},{35,3},{4,36},{36... | collective-permute-start | bytes 7962632 | tf_op jit(solution)/shard_map/ppermute | solution.py:363
  137.4 18.1 %collective-permute-start.12 = (f32[1152,128]{1,0:T(8,128)S(1)}, f32[1152,128]{1,0:T(8,128)S(1)}, u32[]{:S(2)}, u32[]{:S(2)}) collective-permute-start(f32[1152,128]{1,0:T(8,128)S(1)} %stage0.3), channel_id=1, source_target_pairs={{0,192},{1,193},{2,194},{3,195},{4,196},{5,197},{6,198},{7,199},{8... | collective-permute-start | bytes 1769480 | tf_op jit(solution)/shard_map/ppermute | solution.py:403
  138.7 29.3 %collective-permute-start.11 = (f32[1152,128]{1,0:T(8,128)S(1)}, f32[1152,128]{1,0:T(8,128)S(1)}, u32[]{:S(2)}, u32[]{:S(2)}) collective-permute-start(f32[1152,128]{1,0:T(8,128)S(1)} %stage0.3), channel_id=1, source_target_pairs={{0,64},{1,65},{2,66},{3,67},{4,68},{5,69},{6,70},{7,71},{8,72},{9,... | collective-permute-start | bytes 1769480 | tf_op jit(solution)/shard_map/ppermute | solution.py:403
  139.4 35.9 %collective-permute-start.14 = (f32[1152,128]{1,0:T(8,128)S(1)}, f32[1152,128]{1,0:T(8,128)S(1)}, u32[]{:S(2)}, u32[]{:S(2)}) collective-permute-start(f32[1152,128]{1,0:T(8,128)S(1)} %collective-permute-done.9.refs_4_), channel_id=1, source_target_pairs={{192,128},{193,129},{194,130},{195,131},{196,132},{197,133},{198,1... | collective-permute-start | bytes 1769480 | tf_op jit(solution)/shard_map/ppermute | solution.py:403
  155.5 23.2 %collective-permute-start.19 = (f32[1152,128]{1,0:T(8,128)S(1)}, f32[1152,128]{1,0:T(8,128)S(1)}, u32[]{:S(2)}, u32[]{:S(2)}) collective-permute-start(f32[1152,128]{1,0:T(8,128)S(1)} %collective-permute-done.12.refs_4_), channel_id=1, source_target_pairs={{192,128},{193,129},{194,130},{195,131},{196,132},{197,133},{198,1... | collective-permute-start | bytes 1769480 | tf_op jit(solution)/shard_map/ppermute | solution.py:403
  160.5 13.2 %collective-permute-start.13 = (f32[576,1152]{1,0:T(8,128)S(1)}, f32[576,1152]{1,0:T(8,128)S(1)}, u32[]{:S(2)}, u32[]{:S(2)}) collective-permute-start(f32[576,1152]{1,0:T(8,128)S(1)} %order.3.own_ref), channel_id=1, source_target_pairs={{0,32},{32,0},{1,33},{33,1},{2,34},{34,2},{3,35},{35,3},{4,36},{36... | collective-permute-start | bytes 7962632 | tf_op jit(solution)/shard_map/ppermute | solution.py:363
  167.3 8.7 %collective-permute-start.15 = (f32[1152,128]{1,0:T(8,128)S(1)}, f32[1152,128]{1,0:T(8,128)S(1)}, u32[]{:S(2)}, u32[]{:S(2)}) collective-permute-start(f32[1152,128]{1,0:T(8,128)S(1)} %get-tuple-element.28), channel_id=1, source_target_pairs={{64,0},{65,1},{66,2},{67,3},{68,4},{69,5},{70,6},{71,7},{72,8},{73... | collective-permute-start | bytes 1769480 | tf_op jit(solution)/shard_map/ppermute | solution.py:403
  168.0 8.0 %collective-permute-start.16 = (f32[1152,128]{1,0:T(8,128)S(1)}, f32[1152,128]{1,0:T(8,128)S(1)}, u32[]{:S(2)}, u32[]{:S(2)}) collective-permute-start(f32[1152,128]{1,0:T(8,128)S(1)} %get-tuple-element.28), channel_id=1, source_target_pairs={{64,128},{65,129},{66,130},{67,131},{68,132},{69,133},{70,134},{71... | collective-permute-start | bytes 1769480 | tf_op jit(solution)/shard_map/ppermute | solution.py:403
  173.8 4.9 %collective-permute-start.20 = (f32[1152,128]{1,0:T(8,128)S(1)}, f32[1152,128]{1,0:T(8,128)S(1)}, u32[]{:S(2)}, u32[]{:S(2)}) collective-permute-start(f32[1152,128]{1,0:T(8,128)S(1)} %get-tuple-element.29), channel_id=1, source_target_pairs={{64,0},{65,1},{66,2},{67,3},{68,4},{69,5},{70,6},{71,7},{72,8},{73... | collective-permute-start | bytes 1769480 | tf_op jit(solution)/shard_map/ppermute | solution.py:403
  176.1 19.9 %collective-permute-start.17 = (f32[1152,128]{1,0:T(8,128)S(1)}, f32[1152,128]{1,0:T(8,128)S(1)}, u32[]{:S(2)}, u32[]{:S(2)}) collective-permute-start(f32[1152,128]{1,0:T(8,128)S(1)} %stage2.2), channel_id=1, source_target_pairs={{0,192},{1,193},{2,194},{3,195},{4,196},{5,197},{6,198},{7,199},{8... | collective-permute-start | bytes 1769480 | tf_op jit(solution)/shard_map/ppermute | solution.py:403
  177.4 25.2 %collective-permute-start.18 = (f32[1152,128]{1,0:T(8,128)S(1)}, f32[1152,128]{1,0:T(8,128)S(1)}, u32[]{:S(2)}, u32[]{:S(2)}) collective-permute-start(f32[1152,128]{1,0:T(8,128)S(1)} %stage2.2), channel_id=1, source_target_pairs={{128,192},{129,193},{130,194},{131,195},{132,196},{133,197},{134,1... | collective-permute-start | bytes 1769480 | tf_op jit(solution)/shard_map/ppermute | solution.py:403
  178.8 30.6 %collective-permute-start.22 = (f32[1152,128]{1,0:T(8,128)S(1)}, f32[1152,128]{1,0:T(8,128)S(1)}, u32[]{:S(2)}, u32[]{:S(2)}) collective-permute-start(f32[1152,128]{1,0:T(8,128)S(1)} %stage2.3), channel_id=1, source_target_pairs={{0,192},{1,193},{2,194},{3,195},{4,196},{5,197},{6,198},{7,199},{8... | collective-permute-start | bytes 1769480 | tf_op jit(solution)/shard_map/ppermute | solution.py:403
  180.2 35.8 %collective-permute-start.23 = (f32[1152,128]{1,0:T(8,128)S(1)}, f32[1152,128]{1,0:T(8,128)S(1)}, u32[]{:S(2)}, u32[]{:S(2)}) collective-permute-start(f32[1152,128]{1,0:T(8,128)S(1)} %stage2.3), channel_id=1, source_target_pairs={{128,192},{129,193},{130,194},{131,195},{132,196},{133,197},{134,1... | collective-permute-start | bytes 1769480 | tf_op jit(solution)/shard_map/ppermute | solution.py:403
  (25 other events, 188.9 us)
Sparse Core Ops, SparseCore 0:
  31.3 92.0 all-gather.1
where the time goes:
time: 234 us; the launch traced here: 233 us
  waiting for transfers between devices  112 us (48%)
  starting transfers between devices  42.2 us (18%)
  Pallas kernels  37.9 us (16%)
  between operations  18.5 us (8%)
  local copies, waits for them, and re-layouts  18.3 us (8%)
  other arithmetic  2.95 us (1%)
    ppermute x14, waiting for transfers between devices, send(): return lax.ppermute(value, 'y', pairs)  59.3 us
    ppermute x1, waiting for transfers between devices, per_device(): lax.ppermute(near, 'x', ahead)  25.5 us
    pallas_call x8, Pallas kernels, stage(): pl.pallas_call(functools.partial(stage_kernel, rows, number), out_shape=(...  16.2 us
    ppermute x14, starting transfers between devices, send(): return lax.ppermute(value, 'y', pairs)  14.7 us
    all_to_all x1, waiting for transfers between devices, spread(): lax.all_to_all(copies, 'z', 0, 0, tiled=True)  11.4 us
    pallas_call x1, Pallas kernels, per_device(): pl.pallas_call(functools.partial(invert_kernel, rows, xs, zs, tiles), out...  10.6 us
    all_to_all x1, starting transfers between devices, spread(): lax.all_to_all(copies, 'z', 0, 0, tiled=True)  8.19 us
    unnamed x42, local copies, waits for them, and re-layouts  7.76 us
  transfers between devices with their start and end apart: 28, of which 14 were waited for; matrix products, arithmetic and copies ran while one was open for 5% of the time, Pallas kernels for 13%

commit v1 on v0

--- a/solution.py
+++ b/solution.py
@@ -97,13 +97,14 @@
         o_ref[:, tile * LANES : (tile + 1) * LANES] = a_ref[tile, :rows, :]
 
 
-def order_kernel(rows, pieces, pad_rows, first, tiles, whole_ref, o_ref, s_ref):
+def order_kernel(rows, pieces, pad_rows, tiles, whole_ref, o_ref, s_ref):
     per = rows // pieces
+    whole_ref = whole_ref.reshape(pieces * pad_rows, LANES)
     for tile in range(tiles):
 
         def move(row, carry):
             s_ref[pl.ds(row, pieces, stride=per), :] = whole_ref[
-                pl.ds(first + row * tiles + tile, pieces, stride=pad_rows), :
+                pl.ds(row * tiles + tile, pieces, stride=pad_rows), :
             ]
             return carry
 
@@ -373,15 +374,16 @@
 
     def ordered(which, whole, zero):
         own = pl.pallas_call(
-            functools.partial(order_kernel, rows, pieces, 2 * lpad, which * lpad, ltiles),
+            functools.partial(order_kernel, rows, pieces, lpad, ltiles),
             out_shape=jax.ShapeDtypeStruct((rows, span), jnp.float32),
-            in_specs=[here],
+            grid=(1,),
+            in_specs=[pl.BlockSpec((pieces, 1, lpad, LANES), lambda i: (0, which, 0, 0), pipeline_mode=pl.Buffered(1))],
             out_specs=here,
             scratch_shapes=[pltpu.VMEM((rows, LANES), jnp.float32)],
             compiler_params=small,
             cost_estimate=pl.CostEstimate(flops=1_000_000, bytes_accessed=8_000_000, transcendentals=0),
             name="order",
-        )(whole)
+        )(whole.reshape(pieces, 2, lpad, LANES))
         return paired(own, zero)
 
     block = jax.ShapeDtypeStruct((span, LANES), jnp.float32)
@@ -408,14 +410,17 @@
     firsts = [(send(x0, [(0, 1)]), send(x0, [(0, 3)])) for x0 in x0s]
     whole, zero = after(whole, [*firsts[0], x0s[-1]])
     a_mat = ordered(0, whole, zero)
-    x1s, nexts = [], []
+    x1s, nexts, tokens = [], [], []
     for index, (state, (to1, to3)) in enumerate(zip(list(states), firsts)):
+        if index > 0:
+            to1, to3, token = lax.optimization_barrier((to1, to3, x1s[-1][0][:1]))
+            tokens.append(token)
         to2 = send(to3, [(3, 2)])
         states[index], x1 = stage(1, inverse, a_mat, state, to1, to3)
         near_x, to0 = send(x1, [(1, 2)]), send(x1, [(1, 0)])
         x1s.append((x1, to2))
         nexts.append((near_x, to0))
-    _, zero = after(core_arg, [x1 for x1, _ in x1s])
+    _, zero = after(core_arg, [x1 for x1, _ in x1s] + tokens)
     b_mat = ordered(1, whole, zero)
     for state, x0, (x1, to2), (near_x, to0) in zip(states, x0s, x1s, nexts):
         (x2,) = stage(2, inverse, a_mat, b_mat, state, to2, to0, near_x)

time: 234 us -> 222 us (0.949)
  waiting for transfers between devices: 112 us -> 99.5 us
    ppermute x14, waiting for transfers between devices: 59.3 us -> 47.2 us  [send(): return lax.ppermute(value, 'y', pairs)]
  transfers between devices with their start and end apart: 28 -> 28, of which waited for: 14 -> 15; matrix products, arithmetic and copies ran while one was open for 5% -> 5% of each run, Pallas kernels for 13% -> 13%
where the time goes in v1:
time: 222 us; the launch traced here: 221 us
  waiting for transfers between devices  99.5 us (45%)
  starting transfers between devices  41.8 us (19%)
  Pallas kernels  37.8 us (17%)
  local copies, waits for them, and re-layouts  19.1 us (9%)
  between operations  18.5 us (8%)
  other arithmetic  2.94 us (1%)
    ppermute x14, waiting for transfers between devices, send(): return lax.ppermute(value, 'y', pairs)  47.2 us
    ppermute x1, waiting for transfers between devices, per_device(): lax.ppermute(near, 'x', ahead)  25.5 us
    pallas_call x8, Pallas kernels, stage(): pl.pallas_call(functools.partial(stage_kernel, rows, number), out_shape=(...  16.2 us
    ppermute x14, starting transfers between devices, send(): return lax.ppermute(value, 'y', pairs)  14.7 us
    all_to_all x1, waiting for transfers between devices, spread(): lax.all_to_all(copies, 'z', 0, 0, tiled=True)  11.4 us
    pallas_call x1, Pallas kernels, per_device(): pl.pallas_call(functools.partial(invert_kernel, rows, xs, zs, tiles), out...  10.6 us
    unnamed x42, local copies, waits for them, and re-layouts  8.59 us
    all_to_all x1, starting transfers between devices, spread(): lax.all_to_all(copies, 'z', 0, 0, tiled=True)  8.19 us
  transfers between devices with their start and end apart: 28, of which 15 were waited for; matrix products, arithmetic and copies ran while one was open for 5% of the time, Pallas kernels for 13%

profile of v1, /device:TPU:31, one launch (start us, length us, event | category | flops | bytes accessed | tf_op | source)
XLA Modules:
  0.0 221.2 jit_solution(6476396952039083160)
XLA Ops:
  7.5 2.6 %collective-permute-start = (f32[18,288]{1,0:T(8,128)S(1)}, f32[18,288]{1,0:T(8,128)S(1)}, u32[]{:S(2)}, u32[]{:S(2)}) collective-permute-start(f32[18,288]{1,0:T(8,128)S(1)} %get-tuple-element.46), channel_id=1, source_target_pairs={{32,0},{33,1},{34,2},{35,3},{36,4},{37,5},{38,6},{39,7},{40,8},{41... | collective-permute-start | bytes 62216 | tf_op jit(solution)/shard_map/ppermute | solution.py:288
  14.9 8.2 %all-to-all-start = ((f32[8,144,128]{2,1,0:T(8,128)}), f32[8,144,128]{2,1,0:T(8,128)S(1)}, u32[]{:S(2)}, u32[]{:S(2)}) async-start(f32[8,144,128]{2,1,0:T(8,128)} %broadcast_in_dim.8), calls=%async_computation | async-start | bytes 1179648 | tf_op jit(solution)/shard_map/all_to_all | solution.py:298
  23.8 2.5 %collective-permute-start.7 = (f32[18,1152]{1,0:T(8,128)}, f32[18,1152]{1,0:T(8,128)}, u32[]{:S(2)}, u32[]{:S(2)}) collective-permute-start(f32[18,1152]{1,0:T(8,128)} %slice.70), channel_id=1, source_target_pairs={{192,0},{193,1},{194,2},{195,3},{196,4},{197,5},{198,6},{199,7},{2... | collective-permute-start | bytes 248840 | tf_op jit(solution)/shard_map/ppermute | solution.py:313
  31.2 11.4 %all-to-all-done = f32[8,144,128]{2,1,0:T(8,128)S(1)} async-done(((f32[8,144,128]{2,1,0:T(8,128)}), f32[8,144,128]{2,1,0:T(8,128)S(1)}, u32[]{:S(2)}, u32[]{:S(2)}) %all-to-all-start) | async-done | bytes 589856 | tf_op jit(solution)/shard_map/all_to_all | solution.py:298
  42.5 5.7 %all-to-all-start.1 = ((f32[64,8,576]{2,1,0:T(8,128)}), f32[64,8,576]{2,1,0:T(8,128)S(1)}, u32[]{:S(2)}, u32[]{:S(2)}) async-start(f32[64,8,576]{2,1,0:T(8,128)} %copy-done.16), calls=%async_computation.1 | async-start | bytes 2621440 | tf_op jit(solution)/shard_map/all_to_all | solution.py:300
  49.8 25.5 %collective-permute-done.2.left_ref = f32[1152,128]{1,0:T(8,128)S(1)} collective-permute-done((f32[1152,128]{1,0:T(8,128)S(1)}, f32[1152,128]{1,0:T(8,128)S(1)}, u32[]{:S(2)}, u32[]{:S(2)}) %collective-permute-start.2) | collective-permute-done | bytes 589856 | tf_op jit(solution)/shard_map/ppermute | solution.py:316
  80.8 6.7 %collective-permute-done.3.far0_ref = f32[576,128]{1,0:T(8,128)S(1)} collective-permute-done((f32[576,128]{1,0:T(8,128)}, f32[576,128]{1,0:T(8,128)S(1)}, u32[]{:S(2)}, u32[]{:S(2)}) %collective-permute-start.3) | collective-permute-done | bytes 294944 | tf_op jit(solution)/shard_map/ppermute | solution.py:321
  87.5 2.8 %collective-permute-done.5.far1_ref = f32[576,128]{1,0:T(8,128)} collective-permute-done((f32[576,128]{1,0:T(8,128)}, f32[576,128]{1,0:T(8,128)}, u32[]{:S(2)}, u32[]{:S(2)}) %collective-permute-start.5) | collective-permute-done | bytes 294944 | tf_op jit(solution)/shard_map/ppermute | solution.py:321
  92.5 10.6 %invert.1.own_ref = f32[576,1024]{1,0:T(8,128)S(1)} custom-call(s32[1]{0:T(128)S(6)} %add.68.x_ref, f32[1152,128]{1,0:T(8,128)S(1)} %bitcast.28, f32[1152,128]{1,0:T(8,128)S(1)} %copy-done.5, f32[576,128]{1,0:T(8,128)S(1)} %collective-permute-done.3.far0_ref, f32[576,128]{1,0:T(8,128)} %collective-permute-done.5.far1_ref, f32[1152,128]{1,0:T(8,128)S(1)} %copy-done.7), custom_call_target="tpu_custom_call" | custom-call | flops 1000 | bytes 1000 | tf_op jit(solution)/shard_map/invert/pallas_call | solution.py:336
  113.8 14.9 %collective-permute-done.9.refs_4_ = f32[1152,128]{1,0:T(8,128)S(1)} collective-permute-done((f32[1152,128]{1,0:T(8,128)S(1)}, f32[1152,128]{1,0:T(8,128)S(1)}, u32[]{:S(2)}, u32[]{:S(2)}) %collective-permute-start.9) | collective-permute-done | bytes 589856 | tf_op jit(solution)/shard_map/ppermute | solution.py:405
  131.2 2.6 %copy-done.1 = f32[10752,128]{1,0:T(8,128)S(1)} copy-done((f32[10752,128]{1,0:T(8,128)S(1)}, f32[10752,128]{1,0:T(8,128)}, u32[]{:S(2)}) %copy-start.1) | copy-done | bytes 5505048
  133.8 2.6 %order.2.own_ref = f32[576,1152]{1,0:T(8,128)} custom-call(f32[32,2,168,128]{3,2,1,0:T(8,128)S(1)} %bitcast.21), custom_call_target="tpu_custom_call" | custom-call | flops 1000000 | bytes 8000000 | tf_op jit(solution)/shard_map/order/pallas_call | solution.py:376
  140.6 2.6 %copy-done.2 = f32[10752,128]{1,0:T(8,128)S(1)} copy-done((f32[10752,128]{1,0:T(8,128)S(1)}, f32[10752,128]{1,0:T(8,128)}, u32[]{:S(2)}) %copy-start.2) | copy-done | bytes 5505048
  144.2 3.7 %pack.4.refs_1_ = bf16[2,2,576,1152]{3,2,1,0:T(8,128)(2,1)S(1)} custom-call(s32[1]{0:T(128)S(6)} %add.73.core_ref, f32[576,1152]{1,0:T(8,128)} %order.2.own_ref, f32[576,1152]{1,0:T(8,128)} %collective-permute-done.10.other_ref), custom_call_target="tpu_custom_call" | custom-call | flops 1000000 | bytes 8000000 | tf_op jit(solution)/shard_map/pack/pallas_call | solution.py:365
  147.9 2.5 %stage1.2 = (f32[1152,128]{1,0:T(8,128)S(1)}, f32[1152,128]{1,0:T(8,128)S(1)}) custom-call(s32[1]{0:T(128)} %bitcast.plane_ref, bf16[2,2,576,1024]{3,2,1,0:T(8,128)(2,1)S(1)} %bitcast.25, bf16[2,2,576,1152]{3,2,1,0:T(8,128)(2,1)S(1)} %pack.4.refs_1_, f32[1152,128]{1,0:T(8,128)S(1)} %copy-done.13, f32[1152,128]{1,0:T(8,128)S(1)} %copy-done.15, ...), custom_call_target="tpu_custom_call" | custom-call | flops 30000001024 | bytes 4000000 | tf_op jit(solution)/shard_map/stage1/pallas_call | solution.py:393
  151.9 4.1 %collective-permute-done.12.refs_4_ = f32[1152,128]{1,0:T(8,128)S(1)} collective-permute-done((f32[1152,128]{1,0:T(8,128)S(1)}, f32[1152,128]{1,0:T(8,128)S(1)}, u32[]{:S(2)}, u32[]{:S(2)}) %collective-permute-start.12) | collective-permute-done | bytes 589856 | tf_op jit(solution)/shard_map/ppermute | solution.py:405
  156.0 2.7 %stage1.3 = (f32[1152,128]{1,0:T(8,128)S(1)}, f32[1152,128]{1,0:T(8,128)S(1)}) custom-call(s32[1]{0:T(128)} %bitcast.plane_ref, bf16[2,2,576,1024]{3,2,1,0:T(8,128)(2,1)S(1)} %bitcast.25, bf16[2,2,576,1152]{3,2,1,0:T(8,128)(2,1)S(1)} %pack.4.refs_1_, f32[1152,128]{1,0:T(8,128)S(1)} %get-tuple-element.28.refs_1_.refs_2_, ...), custom_call_target="tpu_custom_call" | custom-call | flops 30000001024 | bytes 4000000 | tf_op jit(solution)/shard_map/stage1/pallas_call | solution.py:393
  167.3 9.4 %collective-permute-done.19.refs_4_ = f32[1152,128]{1,0:T(8,128)S(1)} collective-permute-done((f32[1152,128]{1,0:T(8,128)S(1)}, f32[1152,128]{1,0:T(8,128)S(1)}, u32[]{:S(2)}, u32[]{:S(2)}) %collective-permute-start.19) | collective-permute-done | bytes 589856 | tf_op jit(solution)/shard_map/ppermute | solution.py:405
  179.6 5.6 %collective-permute-done.17.refs_3_ = f32[1152,128]{1,0:T(8,128)S(1)} collective-permute-done((f32[1152,128]{1,0:T(8,128)S(1)}, f32[1152,128]{1,0:T(8,128)S(1)}, u32[]{:S(2)}, u32[]{:S(2)}) %collective-permute-start.17) | collective-permute-done | bytes 589856 | tf_op jit(solution)/shard_map/ppermute | solution.py:405
  185.1 5.0 %collective-permute-done.18.refs_4_ = f32[1152,128]{1,0:T(8,128)S(1)} collective-permute-done((f32[1152,128]{1,0:T(8,128)S(1)}, f32[1152,128]{1,0:T(8,128)S(1)}, u32[]{:S(2)}, u32[]{:S(2)}) %collective-permute-start.18) | collective-permute-done | bytes 589856 | tf_op jit(solution)/shard_map/ppermute | solution.py:405
  190.2 5.4 %stage3.2 = f32[1152,128]{1,0:T(8,128)S(1)} custom-call(s32[1]{0:T(128)} %bitcast.plane_ref, bf16[2,2,576,1024]{3,2,1,0:T(8,128)(2,1)S(1)} %bitcast.25, bf16[2,2,576,1152]{3,2,1,0:T(8,128)(2,1)S(1)} %pack.5.refs_2_.refs_1_, f32[1152,128]{1,0:T(8,128)S(1)} %get-tuple-element.37.refs_3_.refs_2_, f32[1152,128]{1,0:T(8,128)S(1)} %collective-permute-done.17.refs_3_, ...), custom_call_target="tpu_custom_call" | custom-call | flops 30000001024 | bytes 4000000 | tf_op jit(solution)/shard_map/stage3/pallas_call | solution.py:393
  195.7 2.7 %collective-permute-done.22.refs_3_ = f32[1152,128]{1,0:T(8,128)S(1)} collective-permute-done((f32[1152,128]{1,0:T(8,128)S(1)}, f32[1152,128]{1,0:T(8,128)S(1)}, u32[]{:S(2)}, u32[]{:S(2)}) %collective-permute-start.22) | collective-permute-done | bytes 589856 | tf_op jit(solution)/shard_map/ppermute | solution.py:405
  198.4 5.5 %collective-permute-done.23.refs_4_ = f32[1152,128]{1,0:T(8,128)S(1)} collective-permute-done((f32[1152,128]{1,0:T(8,128)S(1)}, f32[1152,128]{1,0:T(8,128)S(1)}, u32[]{:S(2)}, u32[]{:S(2)}) %collective-permute-start.23) | collective-permute-done | bytes 589856 | tf_op jit(solution)/shard_map/ppermute | solution.py:405
  203.9 5.4 %stage3.3 = f32[1152,128]{1,0:T(8,128)S(1)} custom-call(s32[1]{0:T(128)} %bitcast.plane_ref, bf16[2,2,576,1024]{3,2,1,0:T(8,128)(2,1)S(1)} %bitcast.25, bf16[2,2,576,1152]{3,2,1,0:T(8,128)(2,1)S(1)} %pack.5.refs_2_.refs_1_, f32[1152,128]{1,0:T(8,128)S(1)} %get-tuple-element.38.refs_3_.refs_2_, f32[1152,128]{1,0:T(8,128)S(1)} %collective-permute-done.22.refs_3_, ...), custom_call_target="tpu_custom_call" | custom-call | flops 30000001024 | bytes 4000000 | tf_op jit(solution)/shard_map/stage3/pallas_call | solution.py:393
  (127 shorter events, 52.2 us)
Async XLA Ops:
  7.5 5.7 %collective-permute-start = (f32[18,288]{1,0:T(8,128)S(1)}, f32[18,288]{1,0:T(8,128)S(1)}, u32[]{:S(2)}, u32[]{:S(2)}) collective-permute-start(f32[18,288]{1,0:T(8,128)S(1)} %get-tuple-element.46), channel_id=1, source_target_pairs={{32,0},{33,1},{34,2},{35,3},{36,4},{37,5},{38,6},{39,7},{40,8},{41... | collective-permute-start | bytes 62216 | tf_op jit(solution)/shard_map/ppermute | solution.py:288
  14.9 27.6 %all-to-all-start = ((f32[8,144,128]{2,1,0:T(8,128)}), f32[8,144,128]{2,1,0:T(8,128)S(1)}, u32[]{:S(2)}, u32[]{:S(2)}) async-start(f32[8,144,128]{2,1,0:T(8,128)} %broadcast_in_dim.8), calls=%async_computation | async-start | bytes 1179648 | tf_op jit(solution)/shard_map/all_to_all | solution.py:298
  23.1 108.1 %all-gather.2.cloned.1.call-start = ((), (), s32[]{:S(2)}) async-start(), calls=%async_computation.2 | async-start | bytes 5677056 | tf_op jit(solution)/shard_map/all_gather | solution.py:317
  42.5 47.7 %all-to-all-start.1 = ((f32[64,8,576]{2,1,0:T(8,128)}), f32[64,8,576]{2,1,0:T(8,128)S(1)}, u32[]{:S(2)}, u32[]{:S(2)}) async-start(f32[64,8,576]{2,1,0:T(8,128)} %copy-done.16), calls=%async_computation.1 | async-start | bytes 2621440 | tf_op jit(solution)/shard_map/all_to_all | solution.py:300
  48.2 27.1 %collective-permute-start.2 = (f32[1152,128]{1,0:T(8,128)S(1)}, f32[1152,128]{1,0:T(8,128)S(1)}, u32[]{:S(2)}, u32[]{:S(2)}) collective-permute-start(f32[1152,128]{1,0:T(8,128)S(1)} %bitcast.26), channel_id=1, source_target_pairs={{0,8},{8,16},{16,24},{24,0},{1,9},{9,17},{17,25},{25,1},{2,10},{10... | collective-permute-start | bytes 1769480 | tf_op jit(solution)/shard_map/ppermute | solution.py:316
  48.3 29.8 %collective-permute-start.4 = (f32[1152,128]{1,0:T(8,128)S(1)}, f32[1152,128]{1,0:T(8,128)S(1)}, u32[]{:S(2)}, u32[]{:S(2)}) collective-permute-start(f32[1152,128]{1,0:T(8,128)S(1)} %bitcast.27), channel_id=1, source_target_pairs={{0,24},{8,0},{16,8},{24,16},{1,25},{9,1},{17,9},{25,17},{2,26},{10... | collective-permute-start | bytes 1769480 | tf_op jit(solution)/shard_map/ppermute | solution.py:316
  76.1 11.4 %collective-permute-start.3 = (f32[576,128]{1,0:T(8,128)}, f32[576,128]{1,0:T(8,128)S(1)}, u32[]{:S(2)}, u32[]{:S(2)}) collective-permute-start(f32[576,128]{1,0:T(8,128)} %slice.82), channel_id=1, source_target_pairs={{0,8},{8,16},{16,24},{24,0},{1,9},{9,17},{17,25},{25,1},{2,10},{10... | collective-permute-start | bytes 884744 | tf_op jit(solution)/shard_map/ppermute | solution.py:321
  79.0 11.3 %collective-permute-start.5 = (f32[576,128]{1,0:T(8,128)}, f32[576,128]{1,0:T(8,128)}, u32[]{:S(2)}, u32[]{:S(2)}) collective-permute-start(f32[576,128]{1,0:T(8,128)} %slice.83), channel_id=1, source_target_pairs={{0,24},{8,0},{16,8},{24,16},{1,25},{9,1},{17,9},{25,17},{2,26},{10... | collective-permute-start | bytes 884744 | tf_op jit(solution)/shard_map/ppermute | solution.py:321
  103.1 5.6 %collective-permute-start.6 = (f32[576,1024]{1,0:T(8,128)S(1)}, f32[576,1024]{1,0:T(8,128)S(1)}, u32[]{:S(2)}, u32[]{:S(2)}) collective-permute-start(f32[576,1024]{1,0:T(8,128)S(1)} %invert.1.own_ref), channel_id=1, source_target_pairs={{0,32},{32,0},{1,33},{33,1},{2,34},{34,2},{3,35},{35,3},{4,36},{36... | collective-permute-start | bytes 7077896 | tf_op jit(solution)/shard_map/ppermute | solution.py:346
  110.2 18.5 %collective-permute-start.9 = (f32[1152,128]{1,0:T(8,128)S(1)}, f32[1152,128]{1,0:T(8,128)S(1)}, u32[]{:S(2)}, u32[]{:S(2)}) collective-permute-start(f32[1152,128]{1,0:T(8,128)S(1)} %stage0.2), channel_id=1, source_target_pairs={{0,192},{1,193},{2,194},{3,195},{4,196},{5,197},{6,198},{7,199},{8... | collective-permute-start | bytes 1769480 | tf_op jit(solution)/shard_map/ppermute | solution.py:405
  136.3 7.9 %collective-permute-start.10 = (f32[576,1152]{1,0:T(8,128)}, f32[576,1152]{1,0:T(8,128)}, u32[]{:S(2)}, u32[]{:S(2)}) collective-permute-start(f32[576,1152]{1,0:T(8,128)} %order.2.own_ref), channel_id=1, source_target_pairs={{0,32},{32,0},{1,33},{33,1},{2,34},{34,2},{3,35},{35,3},{4,36},{36... | collective-permute-start | bytes 7962632 | tf_op jit(solution)/shard_map/ppermute | solution.py:364
  137.2 14.0 %collective-permute-start.11 = (f32[1152,128]{1,0:T(8,128)S(1)}, f32[1152,128]{1,0:T(8,128)S(1)}, u32[]{:S(2)}, u32[]{:S(2)}) collective-permute-start(f32[1152,128]{1,0:T(8,128)S(1)} %stage0.3), channel_id=1, source_target_pairs={{0,64},{1,65},{2,66},{3,67},{4,68},{5,69},{6,70},{7,71},{8,72},{9,... | collective-permute-start | bytes 1769480 | tf_op jit(solution)/shard_map/ppermute | solution.py:405
  137.9 18.1 %collective-permute-start.12 = (f32[1152,128]{1,0:T(8,128)S(1)}, f32[1152,128]{1,0:T(8,128)S(1)}, u32[]{:S(2)}, u32[]{:S(2)}) collective-permute-start(f32[1152,128]{1,0:T(8,128)S(1)} %stage0.3), channel_id=1, source_target_pairs={{0,192},{1,193},{2,194},{3,195},{4,196},{5,197},{6,198},{7,199},{8... | collective-permute-start | bytes 1769480 | tf_op jit(solution)/shard_map/ppermute | solution.py:405
  139.2 24.1 %collective-permute-start.14 = (f32[1152,128]{1,0:T(8,128)S(1)}, f32[1152,128]{1,0:T(8,128)S(1)}, u32[]{:S(2)}, u32[]{:S(2)}) collective-permute-start(f32[1152,128]{1,0:T(8,128)S(1)} %collective-permute-done.9.refs_4_), channel_id=1, source_target_pairs={{192,128},{193,129},{194,130},{195,131},{196,132},{197,133},{198,1... | collective-permute-start | bytes 1769480 | tf_op jit(solution)/shard_map/ppermute | solution.py:405
  144.1 17.7 %collective-permute-start.13 = (f32[576,1152]{1,0:T(8,128)S(1)}, f32[576,1152]{1,0:T(8,128)S(1)}, u32[]{:S(2)}, u32[]{:S(2)}) collective-permute-start(f32[576,1152]{1,0:T(8,128)S(1)} %order.3.own_ref), channel_id=1, source_target_pairs={{0,32},{32,0},{1,33},{33,1},{2,34},{34,2},{3,35},{35,3},{4,36},{36... | collective-permute-start | bytes 7962632 | tf_op jit(solution)/shard_map/ppermute | solution.py:364
  150.5 14.2 %collective-permute-start.15 = (f32[1152,128]{1,0:T(8,128)S(1)}, f32[1152,128]{1,0:T(8,128)S(1)}, u32[]{:S(2)}, u32[]{:S(2)}) collective-permute-start(f32[1152,128]{1,0:T(8,128)S(1)} %get-tuple-element.31), channel_id=1, source_target_pairs={{64,0},{65,1},{66,2},{67,3},{68,4},{69,5},{70,6},{71,7},{72,8},{73... | collective-permute-start | bytes 1769480 | tf_op jit(solution)/shard_map/ppermute | solution.py:405
  151.2 13.5 %collective-permute-start.16 = (f32[1152,128]{1,0:T(8,128)S(1)}, f32[1152,128]{1,0:T(8,128)S(1)}, u32[]{:S(2)}, u32[]{:S(2)}) collective-permute-start(f32[1152,128]{1,0:T(8,128)S(1)} %get-tuple-element.31), channel_id=1, source_target_pairs={{64,128},{65,129},{66,130},{67,131},{68,132},{69,133},{70,134},{71... | collective-permute-start | bytes 1769480 | tf_op jit(solution)/shard_map/ppermute | solution.py:405
  159.8 7.5 %collective-permute-start.20 = (f32[1152,128]{1,0:T(8,128)S(1)}, f32[1152,128]{1,0:T(8,128)S(1)}, u32[]{:S(2)}, u32[]{:S(2)}) collective-permute-start(f32[1152,128]{1,0:T(8,128)S(1)} %get-tuple-element.34), channel_id=1, source_target_pairs={{64,0},{65,1},{66,2},{67,3},{68,4},{69,5},{70,6},{71,7},{72,8},{73... | collective-permute-start | bytes 1769480 | tf_op jit(solution)/shard_map/ppermute | solution.py:405
  161.8 5.5 %collective-permute-start.21 = (f32[1152,128]{1,0:T(8,128)S(1)}, f32[1152,128]{1,0:T(8,128)S(1)}, u32[]{:S(2)}, u32[]{:S(2)}) collective-permute-start(f32[1152,128]{1,0:T(8,128)S(1)} %get-tuple-element.34), channel_id=1, source_target_pairs={{64,128},{65,129},{66,130},{67,131},{68,132},{69,133},{70,134},{71... | collective-permute-start | bytes 1769480 | tf_op jit(solution)/shard_map/ppermute | solution.py:405
  163.3 13.5 %collective-permute-start.19 = (f32[1152,128]{1,0:T(8,128)S(1)}, f32[1152,128]{1,0:T(8,128)S(1)}, u32[]{:S(2)}, u32[]{:S(2)}) collective-permute-start(f32[1152,128]{1,0:T(8,128)S(1)} %collective-permute-done.12.refs_4_), channel_id=1, source_target_pairs={{192,128},{193,129},{194,130},{195,131},{196,132},{197,133},{198,1... | collective-permute-start | bytes 1769480 | tf_op jit(solution)/shard_map/ppermute | solution.py:405
  164.7 20.4 %collective-permute-start.17 = (f32[1152,128]{1,0:T(8,128)S(1)}, f32[1152,128]{1,0:T(8,128)S(1)}, u32[]{:S(2)}, u32[]{:S(2)}) collective-permute-start(f32[1152,128]{1,0:T(8,128)S(1)} %stage2.2), channel_id=1, source_target_pairs={{0,192},{1,193},{2,194},{3,195},{4,196},{5,197},{6,198},{7,199},{8... | collective-permute-start | bytes 1769480 | tf_op jit(solution)/shard_map/ppermute | solution.py:405
  166.0 24.1 %collective-permute-start.18 = (f32[1152,128]{1,0:T(8,128)S(1)}, f32[1152,128]{1,0:T(8,128)S(1)}, u32[]{:S(2)}, u32[]{:S(2)}) collective-permute-start(f32[1152,128]{1,0:T(8,128)S(1)} %stage2.2), channel_id=1, source_target_pairs={{128,192},{129,193},{130,194},{131,195},{132,196},{133,197},{134,1... | collective-permute-start | bytes 1769480 | tf_op jit(solution)/shard_map/ppermute | solution.py:405
  176.8 21.6 %collective-permute-start.22 = (f32[1152,128]{1,0:T(8,128)S(1)}, f32[1152,128]{1,0:T(8,128)S(1)}, u32[]{:S(2)}, u32[]{:S(2)}) collective-permute-start(f32[1152,128]{1,0:T(8,128)S(1)} %stage2.3), channel_id=1, source_target_pairs={{0,192},{1,193},{2,194},{3,195},{4,196},{5,197},{6,198},{7,199},{8... | collective-permute-start | bytes 1769480 | tf_op jit(solution)/shard_map/ppermute | solution.py:405
  178.3 25.6 %collective-permute-start.23 = (f32[1152,128]{1,0:T(8,128)S(1)}, f32[1152,128]{1,0:T(8,128)S(1)}, u32[]{:S(2)}, u32[]{:S(2)}) collective-permute-start(f32[1152,128]{1,0:T(8,128)S(1)} %stage2.3), channel_id=1, source_target_pairs={{128,192},{129,193},{130,194},{131,195},{132,196},{133,197},{134,1... | collective-permute-start | bytes 1769480 | tf_op jit(solution)/shard_map/ppermute | solution.py:405
  (25 other events, 154.0 us)
Sparse Core Ops, SparseCore 0:
  31.3 92.0 all-gather.1

commit v2 on v1

--- a/solution.py
+++ b/solution.py
@@ -276,6 +276,16 @@
     sent = lax.dot_general(spread, right_side, (((1,), (1,)), ((), ())), precision=HI, preferred_element_type=jnp.float32)
     sent = sent.reshape(occ_total, cabs_local, rows)
 
+    def flat(block):
+        return jnp.pad(block.reshape(per * ltiles, LANES), ((0, lpad - per * ltiles), (0, 0)))
+
+    ltiles = span // LANES
+    lpad = (per * ltiles + 7) // 8 * 8
+    moved = lax.ppermute(factor[:, span : 2 * span], "y", [(3, 0)])
+    flat_a = flat(jnp.where(plane == 0, moved, factor[:, :span]))
+    flat_b = flat(lax.dynamic_slice_in_dim(factor, jnp.maximum(plane - 1, 0) * span, span, 1))
+    flats = jnp.concatenate([flat_a, flat_b])
+
     swap = [(0, 1), (1, 0)]
     x_arg = lax.axis_index("x").reshape(1).astype(jnp.int32)
     smem = pl.BlockSpec(memory_space=pltpu.SMEM)
@@ -298,24 +308,14 @@
         return lax.all_to_all(copies, "z", 0, 0, tiled=True).reshape(zs * part.shape[0], LANES)
 
     got = lax.all_to_all(sent, ("core", "x", "z"), 0, 0, tiled=True)
-    marker = lax.ppermute(sent[:1, :, :LANES], "core", swap)
-    piece, marker = lax.optimization_barrier((diag.reshape(per * tiles, LANES), marker))
-    x_arg = x_arg + (marker[0, 0, :1] != marker[0, 0, :1]).astype(jnp.int32)
+    piece = diag.reshape(per * tiles, LANES)
+    piece, flats = lax.optimization_barrier((piece, flats))
+    whole = lax.all_gather(flats, ("x", "z"), axis=0, tiled=True)
     near = spread(piece)
     ahead = [(i, (i + 1) % xs) for i in range(xs)]
     behind = [(i, (i - 1) % xs) for i in range(xs)]
 
-    def flat(block):
-        return jnp.pad(block.reshape(per * ltiles, LANES), ((0, lpad - per * ltiles), (0, 0)))
-
-    ltiles = span // LANES
-    lpad = (per * ltiles + 7) // 8 * 8
-    moved = lax.ppermute(factor[:, span : 2 * span], "y", [(3, 0)])
-    flat_a = flat(jnp.where(plane == 0, moved, factor[:, :span]))
-    flat_b = flat(lax.dynamic_slice_in_dim(factor, jnp.maximum(plane - 1, 0) * span, span, 1))
     left, right = lax.ppermute(near, "x", ahead), lax.ppermute(near, "x", behind)
-    whole = lax.all_gather(jnp.concatenate([flat_a, flat_b]), ("x", "z"), axis=0, tiled=True)
-
     def far(left, right):
         middle = left.shape[0] // 2
         return lax.ppermute(left[:middle], "x", ahead), lax.ppermute(right[middle:], "x", behind)

time: 222 us -> 231 us (1.041)
  waiting for transfers between devices: 99.5 us -> 110 us
    ppermute x14, waiting for transfers between devices: 47.2 us -> 52.7 us  [send(): return lax.ppermute(value, 'y', pairs)]
    all_to_all x1, waiting for transfers between devices: 11.4 us -> 15.9 us  [spread(): lax.all_to_all(copies, 'z', 0, 0, tiled=True)]
    ppermute x1, starting transfers between devices: 1.42 us -> 3.94 us  [per_device(): theirs = lax.ppermute(mine, 'core', swap)]
  transfers between devices with their start and end apart: 28 -> 27, of which waited for: 15 -> 14; matrix products, arithmetic and copies ran while one was open for 5% -> 4% of each run, Pallas kernels for 13% -> 13%
where the time goes in v2:
time: 231 us
  waiting for transfers between devices  110 us (48%)
  starting transfers between devices  43.1 us (19%)
  Pallas kernels  37.8 us (16%)
  local copies, waits for them, and re-layouts  17.3 us (7%)
  between operations  17.2 us (7%)
  matrix products  2.6 us (1%)
    ppermute x14, waiting for transfers between devices, send(): return lax.ppermute(value, 'y', pairs)  52.7 us
    ppermute x1, waiting for transfers between devices, per_device(): lax.ppermute(near, 'x', ahead)  23.5 us
    pallas_call x8, Pallas kernels, stage(): pl.pallas_call(functools.partial(stage_kernel, rows, number), out_shape=(...  16.2 us
    all_to_all x1, waiting for transfers between devices, spread(): lax.all_to_all(copies, 'z', 0, 0, tiled=True)  15.9 us
    ppermute x14, starting transfers between devices, send(): return lax.ppermute(value, 'y', pairs)  14.7 us
    pallas_call x1, Pallas kernels, per_device(): pl.pallas_call(functools.partial(invert_kernel, rows, xs, zs, tiles), out...  10.6 us
    unnamed x42, local copies, waits for them, and re-layouts  8.56 us
    ppermute x1, waiting for transfers between devices, far(): lax.ppermute(left[:middle], 'x', ahead)  8.5 us
  transfers between devices with their start and end apart: 27, of which 14 were waited for; matrix products, arithmetic and copies ran while one was open for 4% of the time, Pallas kernels for 13%

profile of v2, /device:TPU:31, one launch (start us, length us, event | category | flops | bytes accessed | tf_op | source)
XLA Modules:
  0.0 230.6 jit_solution(15014636957585759669)
XLA Ops:
  7.6 2.6 %collective-permute-start = (f32[18,288]{1,0:T(8,128)S(1)}, f32[18,288]{1,0:T(8,128)S(1)}, u32[]{:S(2)}, u32[]{:S(2)}) collective-permute-start(f32[18,288]{1,0:T(8,128)S(1)} %get-tuple-element.46), channel_id=1, source_target_pairs={{32,0},{33,1},{34,2},{35,3},{36,4},{37,5},{38,6},{39,7},{40,8},{41... | collective-permute-start | bytes 62216 | tf_op jit(solution)/shard_map/ppermute | solution.py:298
  17.3 8.2 %all-to-all-start = ((f32[8,144,128]{2,1,0:T(8,128)}), f32[8,144,128]{2,1,0:T(8,128)S(1)}, u32[]{:S(2)}, u32[]{:S(2)}) async-start(f32[8,144,128]{2,1,0:T(8,128)} %broadcast_in_dim.8), calls=%async_computation | async-start | bytes 1179648 | tf_op jit(solution)/shard_map/all_to_all | solution.py:308
  26.4 2.6 %convolution_bitcast_fusion = f32[64,8,576]{2,1,0:T(8,128)} fusion(f32[576,512]{1,0:T(8,128)S(1)} %copy-done, s32[512]{0:T(512)S(1)} %add.65), kind=kOutput, calls=%fused_computation | convolution fusion | flops 1812201472 | bytes 2361344 | tf_op jit(solution)/shard_map/dot_general | solution.py:276
  29.0 15.9 %all-to-all-done = f32[8,144,128]{2,1,0:T(8,128)S(1)} async-done(((f32[8,144,128]{2,1,0:T(8,128)}), f32[8,144,128]{2,1,0:T(8,128)S(1)}, u32[]{:S(2)}, u32[]{:S(2)}) %all-to-all-start) | async-done | bytes 589856 | tf_op jit(solution)/shard_map/all_to_all | solution.py:308
  44.9 5.7 %all-to-all-start.1 = ((f32[64,8,576]{2,1,0:T(8,128)}), f32[64,8,576]{2,1,0:T(8,128)S(1)}, u32[]{:S(2)}, u32[]{:S(2)}) async-start(f32[64,8,576]{2,1,0:T(8,128)} %convolution_bitcast_fusion), calls=%async_computation.1 | async-start | bytes 2621440 | tf_op jit(solution)/shard_map/all_to_all | solution.py:310
  52.1 23.5 %collective-permute-done.2.left_ref = f32[1152,128]{1,0:T(8,128)S(1)} collective-permute-done((f32[1152,128]{1,0:T(8,128)S(1)}, f32[1152,128]{1,0:T(8,128)S(1)}, u32[]{:S(2)}, u32[]{:S(2)}) %collective-permute-start.2) | collective-permute-done | bytes 589856 | tf_op jit(solution)/shard_map/ppermute | solution.py:318
  79.0 8.5 %collective-permute-done.3.far0_ref = f32[576,128]{1,0:T(8,128)S(1)} collective-permute-done((f32[576,128]{1,0:T(8,128)}, f32[576,128]{1,0:T(8,128)S(1)}, u32[]{:S(2)}, u32[]{:S(2)}) %collective-permute-start.3) | collective-permute-done | bytes 294944 | tf_op jit(solution)/shard_map/ppermute | solution.py:321
  87.5 4.3 %collective-permute-done.5.far1_ref = f32[576,128]{1,0:T(8,128)} collective-permute-done((f32[576,128]{1,0:T(8,128)}, f32[576,128]{1,0:T(8,128)}, u32[]{:S(2)}, u32[]{:S(2)}) %collective-permute-start.5) | collective-permute-done | bytes 294944 | tf_op jit(solution)/shard_map/ppermute | solution.py:321
  93.9 10.6 %invert.1.own_ref = f32[576,1024]{1,0:T(8,128)S(1)} custom-call(s32[1]{0:T(128)} %bitcast.2.x_ref, f32[1152,128]{1,0:T(8,128)S(1)} %bitcast.27, f32[1152,128]{1,0:T(8,128)S(1)} %copy-done.5, f32[576,128]{1,0:T(8,128)S(1)} %collective-permute-done.3.far0_ref, f32[576,128]{1,0:T(8,128)} %collective-permute-done.5.far1_ref, f32[1152,128]{1,0:T(8,128)S(1)} %copy-done.7), custom_call_target="tpu_custom_call" | custom-call | flops 1000 | bytes 1000 | tf_op jit(solution)/shard_map/invert/pallas_call | solution.py:336
  104.6 3.9 %collective-permute-start.6 = (f32[576,1024]{1,0:T(8,128)S(1)}, f32[576,1024]{1,0:T(8,128)S(1)}, u32[]{:S(2)}, u32[]{:S(2)}) collective-permute-start(f32[576,1024]{1,0:T(8,128)S(1)} %invert.1.own_ref), channel_id=1, source_target_pairs={{0,32},{32,0},{1,33},{33,1},{2,34},{34,2},{3,35},{35,3},{4,36},{36... | collective-permute-start | bytes 7077896 | tf_op jit(solution)/shard_map/ppermute | solution.py:346
  117.8 20.3 %collective-permute-done.8.refs_4_ = f32[1152,128]{1,0:T(8,128)S(1)} collective-permute-done((f32[1152,128]{1,0:T(8,128)S(1)}, f32[1152,128]{1,0:T(8,128)S(1)}, u32[]{:S(2)}, u32[]{:S(2)}) %collective-permute-start.8) | collective-permute-done | bytes 589856 | tf_op jit(solution)/shard_map/ppermute | solution.py:405
  140.5 2.6 %copy-done.1 = f32[10752,128]{1,0:T(8,128)S(1)} copy-done((f32[10752,128]{1,0:T(8,128)S(1)}, f32[10752,128]{1,0:T(8,128)}, u32[]{:S(2)}) %copy-start.1) | copy-done | bytes 5505048
  143.1 2.6 %order.2.own_ref = f32[576,1152]{1,0:T(8,128)} custom-call(f32[32,2,168,128]{3,2,1,0:T(8,128)S(1)} %bitcast.20), custom_call_target="tpu_custom_call" | custom-call | flops 1000000 | bytes 8000000 | tf_op jit(solution)/shard_map/order/pallas_call | solution.py:376
  149.9 2.6 %copy-done.2 = f32[10752,128]{1,0:T(8,128)S(1)} copy-done((f32[10752,128]{1,0:T(8,128)S(1)}, f32[10752,128]{1,0:T(8,128)}, u32[]{:S(2)}) %copy-start.2) | copy-done | bytes 5505048
  153.5 3.7 %pack.4.refs_1_ = bf16[2,2,576,1152]{3,2,1,0:T(8,128)(2,1)S(1)} custom-call(s32[1]{0:T(128)S(6)} %add.69.core_ref, f32[576,1152]{1,0:T(8,128)} %order.2.own_ref, f32[576,1152]{1,0:T(8,128)} %collective-permute-done.9.other_ref), custom_call_target="tpu_custom_call" | custom-call | flops 1000000 | bytes 8000000 | tf_op jit(solution)/shard_map/pack/pallas_call | solution.py:365
  161.2 4.1 %collective-permute-done.11.refs_4_ = f32[1152,128]{1,0:T(8,128)S(1)} collective-permute-done((f32[1152,128]{1,0:T(8,128)S(1)}, f32[1152,128]{1,0:T(8,128)S(1)}, u32[]{:S(2)}, u32[]{:S(2)}) %collective-permute-start.11) | collective-permute-done | bytes 589856 | tf_op jit(solution)/shard_map/ppermute | solution.py:405
  165.3 2.7 %stage1.3 = (f32[1152,128]{1,0:T(8,128)S(1)}, f32[1152,128]{1,0:T(8,128)S(1)}) custom-call(s32[1]{0:T(128)} %bitcast.plane_ref, bf16[2,2,576,1024]{3,2,1,0:T(8,128)(2,1)S(1)} %bitcast.24, bf16[2,2,576,1152]{3,2,1,0:T(8,128)(2,1)S(1)} %pack.4.refs_1_, f32[1152,128]{1,0:T(8,128)S(1)} %get-tuple-element.28.refs_1_.refs_2_, ...), custom_call_target="tpu_custom_call" | custom-call | flops 30000001024 | bytes 4000000 | tf_op jit(solution)/shard_map/stage1/pallas_call | solution.py:393
  176.8 9.4 %collective-permute-done.18.refs_4_ = f32[1152,128]{1,0:T(8,128)S(1)} collective-permute-done((f32[1152,128]{1,0:T(8,128)S(1)}, f32[1152,128]{1,0:T(8,128)S(1)}, u32[]{:S(2)}, u32[]{:S(2)}) %collective-permute-start.18) | collective-permute-done | bytes 589856 | tf_op jit(solution)/shard_map/ppermute | solution.py:405
  189.0 5.7 %collective-permute-done.16.refs_3_ = f32[1152,128]{1,0:T(8,128)S(1)} collective-permute-done((f32[1152,128]{1,0:T(8,128)S(1)}, f32[1152,128]{1,0:T(8,128)S(1)}, u32[]{:S(2)}, u32[]{:S(2)}) %collective-permute-start.16) | collective-permute-done | bytes 589856 | tf_op jit(solution)/shard_map/ppermute | solution.py:405
  194.7 4.9 %collective-permute-done.17.refs_4_ = f32[1152,128]{1,0:T(8,128)S(1)} collective-permute-done((f32[1152,128]{1,0:T(8,128)S(1)}, f32[1152,128]{1,0:T(8,128)S(1)}, u32[]{:S(2)}, u32[]{:S(2)}) %collective-permute-start.17) | collective-permute-done | bytes 589856 | tf_op jit(solution)/shard_map/ppermute | solution.py:405
  199.6 5.4 %stage3.2 = f32[1152,128]{1,0:T(8,128)S(1)} custom-call(s32[1]{0:T(128)} %bitcast.plane_ref, bf16[2,2,576,1024]{3,2,1,0:T(8,128)(2,1)S(1)} %bitcast.24, bf16[2,2,576,1152]{3,2,1,0:T(8,128)(2,1)S(1)} %pack.5.refs_2_.refs_1_, f32[1152,128]{1,0:T(8,128)S(1)} %get-tuple-element.37.refs_3_.refs_2_, f32[1152,128]{1,0:T(8,128)S(1)} %collective-permute-done.16.refs_3_, ...), custom_call_target="tpu_custom_call" | custom-call | flops 30000001024 | bytes 4000000 | tf_op jit(solution)/shard_map/stage3/pallas_call | solution.py:393
  205.1 2.8 %collective-permute-done.21.refs_3_ = f32[1152,128]{1,0:T(8,128)S(1)} collective-permute-done((f32[1152,128]{1,0:T(8,128)S(1)}, f32[1152,128]{1,0:T(8,128)S(1)}, u32[]{:S(2)}, u32[]{:S(2)}) %collective-permute-start.21) | collective-permute-done | bytes 589856 | tf_op jit(solution)/shard_map/ppermute | solution.py:405
  207.9 5.4 %collective-permute-done.22.refs_4_ = f32[1152,128]{1,0:T(8,128)S(1)} collective-permute-done((f32[1152,128]{1,0:T(8,128)S(1)}, f32[1152,128]{1,0:T(8,128)S(1)}, u32[]{:S(2)}, u32[]{:S(2)}) %collective-permute-start.22) | collective-permute-done | bytes 589856 | tf_op jit(solution)/shard_map/ppermute | solution.py:405
  213.3 5.4 %stage3.3 = f32[1152,128]{1,0:T(8,128)S(1)} custom-call(s32[1]{0:T(128)} %bitcast.plane_ref, bf16[2,2,576,1024]{3,2,1,0:T(8,128)(2,1)S(1)} %bitcast.24, bf16[2,2,576,1152]{3,2,1,0:T(8,128)(2,1)S(1)} %pack.5.refs_2_.refs_1_, f32[1152,128]{1,0:T(8,128)S(1)} %get-tuple-element.38.refs_3_.refs_2_, f32[1152,128]{1,0:T(8,128)S(1)} %collective-permute-done.21.refs_3_, ...), custom_call_target="tpu_custom_call" | custom-call | flops 30000001024 | bytes 4000000 | tf_op jit(solution)/shard_map/stage3/pallas_call | solution.py:393
  (123 shorter events, 50.0 us)
Async XLA Ops:
  7.6 6.6 %collective-permute-start = (f32[18,288]{1,0:T(8,128)S(1)}, f32[18,288]{1,0:T(8,128)S(1)}, u32[]{:S(2)}, u32[]{:S(2)}) collective-permute-start(f32[18,288]{1,0:T(8,128)S(1)} %get-tuple-element.46), channel_id=1, source_target_pairs={{32,0},{33,1},{34,2},{35,3},{36,4},{37,5},{38,6},{39,7},{40,8},{41... | collective-permute-start | bytes 62216 | tf_op jit(solution)/shard_map/ppermute | solution.py:298
  17.3 27.6 %all-to-all-start = ((f32[8,144,128]{2,1,0:T(8,128)}), f32[8,144,128]{2,1,0:T(8,128)S(1)}, u32[]{:S(2)}, u32[]{:S(2)}) async-start(f32[8,144,128]{2,1,0:T(8,128)} %broadcast_in_dim.8), calls=%async_computation | async-start | bytes 1179648 | tf_op jit(solution)/shard_map/all_to_all | solution.py:308
  25.5 115.0 %all-gather.2.cloned.1.call-start = ((), (), s32[]{:S(2)}) async-start(), calls=%async_computation.2 | async-start | bytes 5677056 | tf_op jit(solution)/shard_map/all_gather | solution.py:313
  44.9 46.9 %all-to-all-start.1 = ((f32[64,8,576]{2,1,0:T(8,128)}), f32[64,8,576]{2,1,0:T(8,128)S(1)}, u32[]{:S(2)}, u32[]{:S(2)}) async-start(f32[64,8,576]{2,1,0:T(8,128)} %convolution_bitcast_fusion), calls=%async_computation.1 | async-start | bytes 2621440 | tf_op jit(solution)/shard_map/all_to_all | solution.py:310
  50.6 25.1 %collective-permute-start.2 = (f32[1152,128]{1,0:T(8,128)S(1)}, f32[1152,128]{1,0:T(8,128)S(1)}, u32[]{:S(2)}, u32[]{:S(2)}) collective-permute-start(f32[1152,128]{1,0:T(8,128)S(1)} %bitcast.25), channel_id=1, source_target_pairs={{0,8},{8,16},{16,24},{24,0},{1,9},{9,17},{17,25},{25,1},{2,10},{10... | collective-permute-start | bytes 1769480 | tf_op jit(solution)/shard_map/ppermute | solution.py:318
  50.7 27.4 %collective-permute-start.4 = (f32[1152,128]{1,0:T(8,128)S(1)}, f32[1152,128]{1,0:T(8,128)S(1)}, u32[]{:S(2)}, u32[]{:S(2)}) collective-permute-start(f32[1152,128]{1,0:T(8,128)S(1)} %bitcast.26), channel_id=1, source_target_pairs={{0,24},{8,0},{16,8},{24,16},{1,25},{9,1},{17,9},{25,17},{2,26},{10... | collective-permute-start | bytes 1769480 | tf_op jit(solution)/shard_map/ppermute | solution.py:318
  76.5 11.0 %collective-permute-start.3 = (f32[576,128]{1,0:T(8,128)}, f32[576,128]{1,0:T(8,128)S(1)}, u32[]{:S(2)}, u32[]{:S(2)}) collective-permute-start(f32[576,128]{1,0:T(8,128)} %slice.72), channel_id=1, source_target_pairs={{0,8},{8,16},{16,24},{24,0},{1,9},{9,17},{17,25},{25,1},{2,10},{10... | collective-permute-start | bytes 884744 | tf_op jit(solution)/shard_map/ppermute | solution.py:321
  79.0 12.8 %collective-permute-start.5 = (f32[576,128]{1,0:T(8,128)}, f32[576,128]{1,0:T(8,128)}, u32[]{:S(2)}, u32[]{:S(2)}) collective-permute-start(f32[576,128]{1,0:T(8,128)} %slice.73), channel_id=1, source_target_pairs={{0,24},{8,0},{16,8},{24,16},{1,25},{9,1},{17,9},{25,17},{2,26},{10... | collective-permute-start | bytes 884744 | tf_op jit(solution)/shard_map/ppermute | solution.py:321
  104.6 8.1 %collective-permute-start.6 = (f32[576,1024]{1,0:T(8,128)S(1)}, f32[576,1024]{1,0:T(8,128)S(1)}, u32[]{:S(2)}, u32[]{:S(2)}) collective-permute-start(f32[576,1024]{1,0:T(8,128)S(1)} %invert.1.own_ref), channel_id=1, source_target_pairs={{0,32},{32,0},{1,33},{33,1},{2,34},{34,2},{3,35},{35,3},{4,36},{36... | collective-permute-start | bytes 7077896 | tf_op jit(solution)/shard_map/ppermute | solution.py:346
  114.2 23.9 %collective-permute-start.8 = (f32[1152,128]{1,0:T(8,128)S(1)}, f32[1152,128]{1,0:T(8,128)S(1)}, u32[]{:S(2)}, u32[]{:S(2)}) collective-permute-start(f32[1152,128]{1,0:T(8,128)S(1)} %stage0.2), channel_id=1, source_target_pairs={{0,192},{1,193},{2,194},{3,195},{4,196},{5,197},{6,198},{7,199},{8... | collective-permute-start | bytes 1769480 | tf_op jit(solution)/shard_map/ppermute | solution.py:405
  145.6 7.9 %collective-permute-start.9 = (f32[576,1152]{1,0:T(8,128)}, f32[576,1152]{1,0:T(8,128)}, u32[]{:S(2)}, u32[]{:S(2)}) collective-permute-start(f32[576,1152]{1,0:T(8,128)} %order.2.own_ref), channel_id=1, source_target_pairs={{0,32},{32,0},{1,33},{33,1},{2,34},{34,2},{3,35},{35,3},{4,36},{36... | collective-permute-start | bytes 7962632 | tf_op jit(solution)/shard_map/ppermute | solution.py:364
  146.5 13.9 %collective-permute-start.10 = (f32[1152,128]{1,0:T(8,128)S(1)}, f32[1152,128]{1,0:T(8,128)S(1)}, u32[]{:S(2)}, u32[]{:S(2)}) collective-permute-start(f32[1152,128]{1,0:T(8,128)S(1)} %stage0.3), channel_id=1, source_target_pairs={{0,64},{1,65},{2,66},{3,67},{4,68},{5,69},{6,70},{7,71},{8,72},{9,... | collective-permute-start | bytes 1769480 | tf_op jit(solution)/shard_map/ppermute | solution.py:405
  147.2 18.1 %collective-permute-start.11 = (f32[1152,128]{1,0:T(8,128)S(1)}, f32[1152,128]{1,0:T(8,128)S(1)}, u32[]{:S(2)}, u32[]{:S(2)}) collective-permute-start(f32[1152,128]{1,0:T(8,128)S(1)} %stage0.3), channel_id=1, source_target_pairs={{0,192},{1,193},{2,194},{3,195},{4,196},{5,197},{6,198},{7,199},{8... | collective-permute-start | bytes 1769480 | tf_op jit(solution)/shard_map/ppermute | solution.py:405
  148.5 24.2 %collective-permute-start.13 = (f32[1152,128]{1,0:T(8,128)S(1)}, f32[1152,128]{1,0:T(8,128)S(1)}, u32[]{:S(2)}, u32[]{:S(2)}) collective-permute-start(f32[1152,128]{1,0:T(8,128)S(1)} %collective-permute-done.8.refs_4_), channel_id=1, source_target_pairs={{192,128},{193,129},{194,130},{195,131},{196,132},{197,133},{198,1... | collective-permute-start | bytes 1769480 | tf_op jit(solution)/shard_map/ppermute | solution.py:405
  153.4 17.8 %collective-permute-start.12 = (f32[576,1152]{1,0:T(8,128)S(1)}, f32[576,1152]{1,0:T(8,128)S(1)}, u32[]{:S(2)}, u32[]{:S(2)}) collective-permute-start(f32[576,1152]{1,0:T(8,128)S(1)} %order.3.own_ref), channel_id=1, source_target_pairs={{0,32},{32,0},{1,33},{33,1},{2,34},{34,2},{3,35},{35,3},{4,36},{36... | collective-permute-start | bytes 7962632 | tf_op jit(solution)/shard_map/ppermute | solution.py:364
  159.8 14.3 %collective-permute-start.14 = (f32[1152,128]{1,0:T(8,128)S(1)}, f32[1152,128]{1,0:T(8,128)S(1)}, u32[]{:S(2)}, u32[]{:S(2)}) collective-permute-start(f32[1152,128]{1,0:T(8,128)S(1)} %get-tuple-element.31), channel_id=1, source_target_pairs={{64,0},{65,1},{66,2},{67,3},{68,4},{69,5},{70,6},{71,7},{72,8},{73... | collective-permute-start | bytes 1769480 | tf_op jit(solution)/shard_map/ppermute | solution.py:405
  160.5 13.6 %collective-permute-start.15 = (f32[1152,128]{1,0:T(8,128)S(1)}, f32[1152,128]{1,0:T(8,128)S(1)}, u32[]{:S(2)}, u32[]{:S(2)}) collective-permute-start(f32[1152,128]{1,0:T(8,128)S(1)} %get-tuple-element.31), channel_id=1, source_target_pairs={{64,128},{65,129},{66,130},{67,131},{68,132},{69,133},{70,134},{71... | collective-permute-start | bytes 1769480 | tf_op jit(solution)/shard_map/ppermute | solution.py:405
  169.2 7.6 %collective-permute-start.19 = (f32[1152,128]{1,0:T(8,128)S(1)}, f32[1152,128]{1,0:T(8,128)S(1)}, u32[]{:S(2)}, u32[]{:S(2)}) collective-permute-start(f32[1152,128]{1,0:T(8,128)S(1)} %get-tuple-element.34), channel_id=1, source_target_pairs={{64,0},{65,1},{66,2},{67,3},{68,4},{69,5},{70,6},{71,7},{72,8},{73... | collective-permute-start | bytes 1769480 | tf_op jit(solution)/shard_map/ppermute | solution.py:405
  171.2 5.5 %collective-permute-start.20 = (f32[1152,128]{1,0:T(8,128)S(1)}, f32[1152,128]{1,0:T(8,128)S(1)}, u32[]{:S(2)}, u32[]{:S(2)}) collective-permute-start(f32[1152,128]{1,0:T(8,128)S(1)} %get-tuple-element.34), channel_id=1, source_target_pairs={{64,128},{65,129},{66,130},{67,131},{68,132},{69,133},{70,134},{71... | collective-permute-start | bytes 1769480 | tf_op jit(solution)/shard_map/ppermute | solution.py:405
  172.7 13.5 %collective-permute-start.18 = (f32[1152,128]{1,0:T(8,128)S(1)}, f32[1152,128]{1,0:T(8,128)S(1)}, u32[]{:S(2)}, u32[]{:S(2)}) collective-permute-start(f32[1152,128]{1,0:T(8,128)S(1)} %collective-permute-done.11.refs_4_), channel_id=1, source_target_pairs={{192,128},{193,129},{194,130},{195,131},{196,132},{197,133},{198,1... | collective-permute-start | bytes 1769480 | tf_op jit(solution)/shard_map/ppermute | solution.py:405
  174.1 20.5 %collective-permute-start.16 = (f32[1152,128]{1,0:T(8,128)S(1)}, f32[1152,128]{1,0:T(8,128)S(1)}, u32[]{:S(2)}, u32[]{:S(2)}) collective-permute-start(f32[1152,128]{1,0:T(8,128)S(1)} %stage2.2), channel_id=1, source_target_pairs={{0,192},{1,193},{2,194},{3,195},{4,196},{5,197},{6,198},{7,199},{8... | collective-permute-start | bytes 1769480 | tf_op jit(solution)/shard_map/ppermute | solution.py:405
  175.4 24.1 %collective-permute-start.17 = (f32[1152,128]{1,0:T(8,128)S(1)}, f32[1152,128]{1,0:T(8,128)S(1)}, u32[]{:S(2)}, u32[]{:S(2)}) collective-permute-start(f32[1152,128]{1,0:T(8,128)S(1)} %stage2.2), channel_id=1, source_target_pairs={{128,192},{129,193},{130,194},{131,195},{132,196},{133,197},{134,1... | collective-permute-start | bytes 1769480 | tf_op jit(solution)/shard_map/ppermute | solution.py:405
  186.2 21.7 %collective-permute-start.21 = (f32[1152,128]{1,0:T(8,128)S(1)}, f32[1152,128]{1,0:T(8,128)S(1)}, u32[]{:S(2)}, u32[]{:S(2)}) collective-permute-start(f32[1152,128]{1,0:T(8,128)S(1)} %stage2.3), channel_id=1, source_target_pairs={{0,192},{1,193},{2,194},{3,195},{4,196},{5,197},{6,198},{7,199},{8... | collective-permute-start | bytes 1769480 | tf_op jit(solution)/shard_map/ppermute | solution.py:405
  187.7 25.6 %collective-permute-start.22 = (f32[1152,128]{1,0:T(8,128)S(1)}, f32[1152,128]{1,0:T(8,128)S(1)}, u32[]{:S(2)}, u32[]{:S(2)}) collective-permute-start(f32[1152,128]{1,0:T(8,128)S(1)} %stage2.3), channel_id=1, source_target_pairs={{128,192},{129,193},{130,194},{131,195},{132,196},{133,197},{134,1... | collective-permute-start | bytes 1769480 | tf_op jit(solution)/shard_map/ppermute | solution.py:405
  (24 other events, 163.0 us)
Sparse Core Ops, SparseCore 0:
  28.9 93.0 all-gather.1

commit v3 on v2

--- a/solution.py
+++ b/solution.py
@@ -309,7 +309,6 @@
 
     got = lax.all_to_all(sent, ("core", "x", "z"), 0, 0, tiled=True)
     piece = diag.reshape(per * tiles, LANES)
-    piece, flats = lax.optimization_barrier((piece, flats))
     whole = lax.all_gather(flats, ("x", "z"), axis=0, tiled=True)
     near = spread(piece)
     ahead = [(i, (i + 1) % xs) for i in range(xs)]
@@ -407,9 +406,11 @@
     x0s, chunks = [], []
     for state in states:
         x0s += stage(0, inverse, state)
-    firsts = [(send(x0, [(0, 1)]), send(x0, [(0, 3)])) for x0 in x0s]
-    whole, zero = after(whole, [*firsts[0], x0s[-1]])
-    a_mat = ordered(0, whole, zero)
+    firsts = [(send(x0, [(0, 1)]), send(x0, [(0, 3)])) for x0 in x0s[:1]] + [None]
+    whole, *first, x0s[-1] = lax.optimization_barrier((whole, *firsts[0], x0s[-1]))
+    firsts[0] = tuple(first)
+    firsts[-1] = send(x0s[-1], [(0, 1)]), send(x0s[-1], [(0, 3)])
+    a_mat = ordered(0, whole, 0)
     x1s, nexts, tokens = [], [], []
     for index, (state, (to1, to3)) in enumerate(zip(list(states), firsts)):
         if index > 0:

time: 231 us -> 221 us (0.957)
  waiting for transfers between devices: 110 us -> 102 us
    ppermute x14, waiting for transfers between devices: 52.7 us -> 46.6 us  [send(): return lax.ppermute(value, 'y', pairs)]
  transfers between devices with their start and end apart: 27 -> 27, of which waited for: 14 -> 13; matrix products, arithmetic and copies ran while one was open for 4% -> 4% of each run, Pallas kernels for 13% -> 13%
where the time goes in v3:
time: 221 us; the launch traced here: 220 us
  waiting for transfers between devices  102 us (46%)
  starting transfers between devices  44.3 us (20%)
  Pallas kernels  37.4 us (17%)
  local copies, waits for them, and re-layouts  15.7 us (7%)
  between operations  15.4 us (7%)
  matrix products  2.6 us (1%)
  other arithmetic  2.28 us (1%)
    ppermute x14, waiting for transfers between devices, send(): return lax.ppermute(value, 'y', pairs)  46.6 us
    ppermute x1, waiting for transfers between devices, per_device(): lax.ppermute(near, 'x', ahead)  23.1 us
    pallas_call x8, Pallas kernels, stage(): pl.pallas_call(functools.partial(stage_kernel, rows, number), out_shape=(...  16.2 us
    all_to_all x1, waiting for transfers between devices, spread(): lax.all_to_all(copies, 'z', 0, 0, tiled=True)  15.6 us
    ppermute x14, starting transfers between devices, send(): return lax.ppermute(value, 'y', pairs)  14.8 us
    pallas_call x1, Pallas kernels, per_device(): pl.pallas_call(functools.partial(invert_kernel, rows, xs, zs, tiles), out...  10.6 us
    ppermute x1, waiting for transfers between devices, far(): lax.ppermute(left[:middle], 'x', ahead)  9.22 us
    unnamed x42, local copies, waits for them, and re-layouts  8.58 us
  transfers between devices with their start and end apart: 27, of which 13 were waited for; matrix products, arithmetic and copies ran while one was open for 4% of the time, Pallas kernels for 13%

profile of v3, /device:TPU:31, one launch (start us, length us, event | category | flops | bytes accessed | tf_op | source)
XLA Modules:
  0.0 219.8 jit_solution(10288324330288559642)
XLA Ops:
  7.5 2.6 %collective-permute-start = (f32[18,288]{1,0:T(8,128)S(1)}, f32[18,288]{1,0:T(8,128)S(1)}, u32[]{:S(2)}, u32[]{:S(2)}) collective-permute-start(f32[18,288]{1,0:T(8,128)S(1)} %get-tuple-element.44), channel_id=1, source_target_pairs={{32,0},{33,1},{34,2},{35,3},{36,4},{37,5},{38,6},{39,7},{40,8},{41... | collective-permute-start | bytes 62216 | tf_op jit(solution)/shard_map/ppermute | solution.py:298
  15.1 8.2 %all-to-all-start = ((f32[8,144,128]{2,1,0:T(8,128)}), f32[8,144,128]{2,1,0:T(8,128)S(1)}, u32[]{:S(2)}, u32[]{:S(2)}) async-start(f32[8,144,128]{2,1,0:T(8,128)} %broadcast_in_dim.8), calls=%async_computation | async-start | bytes 1179648 | tf_op jit(solution)/shard_map/all_to_all | solution.py:308
  24.6 2.6 %convolution_bitcast_fusion = f32[64,8,576]{2,1,0:T(8,128)} fusion(f32[576,512]{1,0:T(8,128)S(1)} %copy-done, s32[512]{0:T(512)S(1)} %add.51), kind=kOutput, calls=%fused_computation | convolution fusion | flops 1812201472 | bytes 2361344 | tf_op jit(solution)/shard_map/dot_general | solution.py:276
  27.2 15.6 %all-to-all-done = f32[8,144,128]{2,1,0:T(8,128)S(1)} async-done(((f32[8,144,128]{2,1,0:T(8,128)}), f32[8,144,128]{2,1,0:T(8,128)S(1)}, u32[]{:S(2)}, u32[]{:S(2)}) %all-to-all-start) | async-done | bytes 589856 | tf_op jit(solution)/shard_map/all_to_all | solution.py:308
  42.7 5.6 %all-to-all-start.1 = ((f32[64,8,576]{2,1,0:T(8,128)}), f32[64,8,576]{2,1,0:T(8,128)S(1)}, u32[]{:S(2)}, u32[]{:S(2)}) async-start(f32[64,8,576]{2,1,0:T(8,128)} %convolution_bitcast_fusion), calls=%async_computation.1 | async-start | bytes 2621440 | tf_op jit(solution)/shard_map/all_to_all | solution.py:310
  49.9 23.1 %collective-permute-done.1.left_ref = f32[1152,128]{1,0:T(8,128)S(1)} collective-permute-done((f32[1152,128]{1,0:T(8,128)S(1)}, f32[1152,128]{1,0:T(8,128)S(1)}, u32[]{:S(2)}, u32[]{:S(2)}) %collective-permute-start.1) | collective-permute-done | bytes 589856 | tf_op jit(solution)/shard_map/ppermute | solution.py:317
  77.2 9.2 %collective-permute-done.2.far0_ref = f32[576,128]{1,0:T(8,128)S(1)} collective-permute-done((f32[576,128]{1,0:T(8,128)}, f32[576,128]{1,0:T(8,128)S(1)}, u32[]{:S(2)}, u32[]{:S(2)}) %collective-permute-start.2) | collective-permute-done | bytes 294944 | tf_op jit(solution)/shard_map/ppermute | solution.py:320
  86.4 4.2 %collective-permute-done.4.far1_ref = f32[576,128]{1,0:T(8,128)} collective-permute-done((f32[576,128]{1,0:T(8,128)}, f32[576,128]{1,0:T(8,128)}, u32[]{:S(2)}, u32[]{:S(2)}) %collective-permute-start.4) | collective-permute-done | bytes 294944 | tf_op jit(solution)/shard_map/ppermute | solution.py:320
  92.7 10.6 %invert.1.own_ref = f32[576,1024]{1,0:T(8,128)S(1)} custom-call(s32[1]{0:T(128)} %bitcast.2.x_ref, f32[1152,128]{1,0:T(8,128)S(1)} %bitcast.26, f32[1152,128]{1,0:T(8,128)S(1)} %copy-done.5, f32[576,128]{1,0:T(8,128)S(1)} %collective-permute-done.2.far0_ref, f32[576,128]{1,0:T(8,128)} %collective-permute-done.4.far1_ref, f32[1152,128]{1,0:T(8,128)S(1)} %copy-done.7), custom_call_target="tpu_custom_call" | custom-call | flops 1000 | bytes 1000 | tf_op jit(solution)/shard_map/invert/pallas_call | solution.py:335
  103.4 3.8 %collective-permute-start.5 = (f32[576,1024]{1,0:T(8,128)S(1)}, f32[576,1024]{1,0:T(8,128)S(1)}, u32[]{:S(2)}, u32[]{:S(2)}) collective-permute-start(f32[576,1024]{1,0:T(8,128)S(1)} %invert.1.own_ref), channel_id=1, source_target_pairs={{0,32},{32,0},{1,33},{33,1},{2,34},{34,2},{3,35},{35,3},{4,36},{36... | collective-permute-start | bytes 7077896 | tf_op jit(solution)/shard_map/ppermute | solution.py:345
  115.4 15.2 %collective-permute-done.8.refs_4_ = f32[1152,128]{1,0:T(8,128)S(1)} collective-permute-done((f32[1152,128]{1,0:T(8,128)S(1)}, f32[1152,128]{1,0:T(8,128)S(1)}, u32[]{:S(2)}, u32[]{:S(2)}) %collective-permute-start.8) | collective-permute-done | bytes 589856 | tf_op jit(solution)/shard_map/ppermute | solution.py:404
  130.6 2.6 %copy-done.1 = f32[10752,128]{1,0:T(8,128)S(1)} copy-done((f32[10752,128]{1,0:T(8,128)S(1)}, f32[10752,128]{1,0:T(8,128)}, u32[]{:S(2)}) %copy-start.1) | copy-done | bytes 5505048
  133.1 2.6 %order.2.own_ref = f32[576,1152]{1,0:T(8,128)} custom-call(f32[32,2,168,128]{3,2,1,0:T(8,128)S(1)} %bitcast.19), custom_call_target="tpu_custom_call" | custom-call | flops 1000000 | bytes 8000000 | tf_op jit(solution)/shard_map/order/pallas_call | solution.py:375
  138.9 2.6 %copy-done.2 = f32[10752,128]{1,0:T(8,128)S(1)} copy-done((f32[10752,128]{1,0:T(8,128)S(1)}, f32[10752,128]{1,0:T(8,128)}, u32[]{:S(2)}) %copy-start.2) | copy-done | bytes 5505048
  144.0 3.3 %pack.4.refs_1_ = bf16[2,2,576,1152]{3,2,1,0:T(8,128)(2,1)S(1)} custom-call(s32[1]{0:T(128)} %bitcast.1.core_ref, f32[576,1152]{1,0:T(8,128)} %order.2.own_ref, f32[576,1152]{1,0:T(8,128)} %collective-permute-done.9.other_ref), custom_call_target="tpu_custom_call" | custom-call | flops 1000000 | bytes 8000000 | tf_op jit(solution)/shard_map/pack/pallas_call | solution.py:364
  147.4 2.5 %stage1.2 = (f32[1152,128]{1,0:T(8,128)S(1)}, f32[1152,128]{1,0:T(8,128)S(1)}) custom-call(s32[1]{0:T(128)} %bitcast.plane_ref, bf16[2,2,576,1024]{3,2,1,0:T(8,128)(2,1)S(1)} %bitcast.23, bf16[2,2,576,1152]{3,2,1,0:T(8,128)(2,1)S(1)} %pack.4.refs_1_, f32[1152,128]{1,0:T(8,128)S(1)} %copy-done.13, f32[1152,128]{1,0:T(8,128)S(1)} %copy-done.15, ...), custom_call_target="tpu_custom_call" | custom-call | flops 30000001024 | bytes 4000000 | tf_op jit(solution)/shard_map/stage1/pallas_call | solution.py:392
  151.3 4.4 %collective-permute-done.11.refs_4_ = f32[1152,128]{1,0:T(8,128)S(1)} collective-permute-done((f32[1152,128]{1,0:T(8,128)S(1)}, f32[1152,128]{1,0:T(8,128)S(1)}, u32[]{:S(2)}, u32[]{:S(2)}) %collective-permute-start.11) | collective-permute-done | bytes 589856 | tf_op jit(solution)/shard_map/ppermute | solution.py:404
  155.7 2.7 %stage1.3 = (f32[1152,128]{1,0:T(8,128)S(1)}, f32[1152,128]{1,0:T(8,128)S(1)}) custom-call(s32[1]{0:T(128)} %bitcast.plane_ref, bf16[2,2,576,1024]{3,2,1,0:T(8,128)(2,1)S(1)} %bitcast.23, bf16[2,2,576,1152]{3,2,1,0:T(8,128)(2,1)S(1)} %pack.4.refs_1_, f32[1152,128]{1,0:T(8,128)S(1)} %get-tuple-element.26.refs_1_.refs_2_, ...), custom_call_target="tpu_custom_call" | custom-call | flops 30000001024 | bytes 4000000 | tf_op jit(solution)/shard_map/stage1/pallas_call | solution.py:392
  167.2 9.4 %collective-permute-done.18.refs_4_ = f32[1152,128]{1,0:T(8,128)S(1)} collective-permute-done((f32[1152,128]{1,0:T(8,128)S(1)}, f32[1152,128]{1,0:T(8,128)S(1)}, u32[]{:S(2)}, u32[]{:S(2)}) %collective-permute-start.18) | collective-permute-done | bytes 589856 | tf_op jit(solution)/shard_map/ppermute | solution.py:404
  179.4 3.6 %collective-permute-done.16.refs_3_ = f32[1152,128]{1,0:T(8,128)S(1)} collective-permute-done((f32[1152,128]{1,0:T(8,128)S(1)}, f32[1152,128]{1,0:T(8,128)S(1)}, u32[]{:S(2)}, u32[]{:S(2)}) %collective-permute-start.16) | collective-permute-done | bytes 589856 | tf_op jit(solution)/shard_map/ppermute | solution.py:404
  183.0 5.8 %collective-permute-done.17.refs_4_ = f32[1152,128]{1,0:T(8,128)S(1)} collective-permute-done((f32[1152,128]{1,0:T(8,128)S(1)}, f32[1152,128]{1,0:T(8,128)S(1)}, u32[]{:S(2)}, u32[]{:S(2)}) %collective-permute-start.17) | collective-permute-done | bytes 589856 | tf_op jit(solution)/shard_map/ppermute | solution.py:404
  188.8 5.4 %stage3.2 = f32[1152,128]{1,0:T(8,128)S(1)} custom-call(s32[1]{0:T(128)} %bitcast.plane_ref, bf16[2,2,576,1024]{3,2,1,0:T(8,128)(2,1)S(1)} %bitcast.23, bf16[2,2,576,1152]{3,2,1,0:T(8,128)(2,1)S(1)} %pack.5.refs_2_.refs_1_, f32[1152,128]{1,0:T(8,128)S(1)} %get-tuple-element.37.refs_3_.refs_2_, f32[1152,128]{1,0:T(8,128)S(1)} %collective-permute-done.16.refs_3_, ...), custom_call_target="tpu_custom_call" | custom-call | flops 30000001024 | bytes 4000000 | tf_op jit(solution)/shard_map/stage3/pallas_call | solution.py:392
  196.4 6.1 %collective-permute-done.22.refs_4_ = f32[1152,128]{1,0:T(8,128)S(1)} collective-permute-done((f32[1152,128]{1,0:T(8,128)S(1)}, f32[1152,128]{1,0:T(8,128)S(1)}, u32[]{:S(2)}, u32[]{:S(2)}) %collective-permute-start.22) | collective-permute-done | bytes 589856 | tf_op jit(solution)/shard_map/ppermute | solution.py:404
  202.6 5.4 %stage3.3 = f32[1152,128]{1,0:T(8,128)S(1)} custom-call(s32[1]{0:T(128)} %bitcast.plane_ref, bf16[2,2,576,1024]{3,2,1,0:T(8,128)(2,1)S(1)} %bitcast.23, bf16[2,2,576,1152]{3,2,1,0:T(8,128)(2,1)S(1)} %pack.5.refs_2_.refs_1_, f32[1152,128]{1,0:T(8,128)S(1)} %get-tuple-element.38.refs_3_.refs_2_, f32[1152,128]{1,0:T(8,128)S(1)} %collective-permute-done.21.refs_3_, ...), custom_call_target="tpu_custom_call" | custom-call | flops 30000001024 | bytes 4000000 | tf_op jit(solution)/shard_map/stage3/pallas_call | solution.py:392
  (120 shorter events, 47.4 us)
Async XLA Ops:
  7.5 6.6 %collective-permute-start = (f32[18,288]{1,0:T(8,128)S(1)}, f32[18,288]{1,0:T(8,128)S(1)}, u32[]{:S(2)}, u32[]{:S(2)}) collective-permute-start(f32[18,288]{1,0:T(8,128)S(1)} %get-tuple-element.44), channel_id=1, source_target_pairs={{32,0},{33,1},{34,2},{35,3},{36,4},{37,5},{38,6},{39,7},{40,8},{41... | collective-permute-start | bytes 62216 | tf_op jit(solution)/shard_map/ppermute | solution.py:298
  11.0 12.6 %collective-permute-start.6 = (f32[18,1152]{1,0:T(8,128)S(1)}, f32[18,1152]{1,0:T(8,128)S(1)}, u32[]{:S(2)}, u32[]{:S(2)}) collective-permute-start(f32[18,1152]{1,0:T(8,128)S(1)} %slice.52), channel_id=1, source_target_pairs={{192,0},{193,1},{194,2},{195,3},{196,4},{197,5},{198,6},{199,7},{2... | collective-permute-start | bytes 248840 | tf_op jit(solution)/shard_map/ppermute | solution.py:284
  15.1 27.7 %all-to-all-start = ((f32[8,144,128]{2,1,0:T(8,128)}), f32[8,144,128]{2,1,0:T(8,128)S(1)}, u32[]{:S(2)}, u32[]{:S(2)}) async-start(f32[8,144,128]{2,1,0:T(8,128)} %broadcast_in_dim.8), calls=%async_computation | async-start | bytes 1179648 | tf_op jit(solution)/shard_map/all_to_all | solution.py:308
  23.3 107.3 %all-gather.2.cloned.1.call-start = ((), (), s32[]{:S(2)}) async-start(), calls=%async_computation.2 | async-start | bytes 5677056 | tf_op jit(solution)/shard_map/all_gather | solution.py:312
  42.7 47.9 %all-to-all-start.1 = ((f32[64,8,576]{2,1,0:T(8,128)}), f32[64,8,576]{2,1,0:T(8,128)S(1)}, u32[]{:S(2)}, u32[]{:S(2)}) async-start(f32[64,8,576]{2,1,0:T(8,128)} %convolution_bitcast_fusion), calls=%async_computation.1 | async-start | bytes 2621440 | tf_op jit(solution)/shard_map/all_to_all | solution.py:310
  48.4 24.6 %collective-permute-start.1 = (f32[1152,128]{1,0:T(8,128)S(1)}, f32[1152,128]{1,0:T(8,128)S(1)}, u32[]{:S(2)}, u32[]{:S(2)}) collective-permute-start(f32[1152,128]{1,0:T(8,128)S(1)} %bitcast.24), channel_id=1, source_target_pairs={{0,8},{8,16},{16,24},{24,0},{1,9},{9,17},{17,25},{25,1},{2,10},{10... | collective-permute-start | bytes 1769480 | tf_op jit(solution)/shard_map/ppermute | solution.py:317
  48.5 27.8 %collective-permute-start.3 = (f32[1152,128]{1,0:T(8,128)S(1)}, f32[1152,128]{1,0:T(8,128)S(1)}, u32[]{:S(2)}, u32[]{:S(2)}) collective-permute-start(f32[1152,128]{1,0:T(8,128)S(1)} %bitcast.25), channel_id=1, source_target_pairs={{0,24},{8,0},{16,8},{24,16},{1,25},{9,1},{17,9},{25,17},{2,26},{10... | collective-permute-start | bytes 1769480 | tf_op jit(solution)/shard_map/ppermute | solution.py:317
  73.8 12.6 %collective-permute-start.2 = (f32[576,128]{1,0:T(8,128)}, f32[576,128]{1,0:T(8,128)S(1)}, u32[]{:S(2)}, u32[]{:S(2)}) collective-permute-start(f32[576,128]{1,0:T(8,128)} %slice.60), channel_id=1, source_target_pairs={{0,8},{8,16},{16,24},{24,0},{1,9},{9,17},{17,25},{25,1},{2,10},{10... | collective-permute-start | bytes 884744 | tf_op jit(solution)/shard_map/ppermute | solution.py:320
  77.2 13.4 %collective-permute-start.4 = (f32[576,128]{1,0:T(8,128)}, f32[576,128]{1,0:T(8,128)}, u32[]{:S(2)}, u32[]{:S(2)}) collective-permute-start(f32[576,128]{1,0:T(8,128)} %slice.61), channel_id=1, source_target_pairs={{0,24},{8,0},{16,8},{24,16},{1,25},{9,1},{17,9},{25,17},{2,26},{10... | collective-permute-start | bytes 884744 | tf_op jit(solution)/shard_map/ppermute | solution.py:320
  103.4 8.0 %collective-permute-start.5 = (f32[576,1024]{1,0:T(8,128)S(1)}, f32[576,1024]{1,0:T(8,128)S(1)}, u32[]{:S(2)}, u32[]{:S(2)}) collective-permute-start(f32[576,1024]{1,0:T(8,128)S(1)} %invert.1.own_ref), channel_id=1, source_target_pairs={{0,32},{32,0},{1,33},{33,1},{2,34},{34,2},{3,35},{35,3},{4,36},{36... | collective-permute-start | bytes 7077896 | tf_op jit(solution)/shard_map/ppermute | solution.py:345
  112.9 17.6 %collective-permute-start.8 = (f32[1152,128]{1,0:T(8,128)S(1)}, f32[1152,128]{1,0:T(8,128)S(1)}, u32[]{:S(2)}, u32[]{:S(2)}) collective-permute-start(f32[1152,128]{1,0:T(8,128)S(1)} %stage0.2), channel_id=1, source_target_pairs={{0,192},{1,193},{2,194},{3,195},{4,196},{5,197},{6,198},{7,199},{8... | collective-permute-start | bytes 1769480 | tf_op jit(solution)/shard_map/ppermute | solution.py:404
  135.7 8.3 %collective-permute-start.9 = (f32[576,1152]{1,0:T(8,128)}, f32[576,1152]{1,0:T(8,128)}, u32[]{:S(2)}, u32[]{:S(2)}) collective-permute-start(f32[576,1152]{1,0:T(8,128)} %order.2.own_ref), channel_id=1, source_target_pairs={{0,32},{32,0},{1,33},{33,1},{2,34},{34,2},{3,35},{35,3},{4,36},{36... | collective-permute-start | bytes 7962632 | tf_op jit(solution)/shard_map/ppermute | solution.py:363
  136.9 13.7 %collective-permute-start.10 = (f32[1152,128]{1,0:T(8,128)S(1)}, f32[1152,128]{1,0:T(8,128)S(1)}, u32[]{:S(2)}, u32[]{:S(2)}) collective-permute-start(f32[1152,128]{1,0:T(8,128)S(1)} %stage0.3), channel_id=1, source_target_pairs={{0,64},{1,65},{2,66},{3,67},{4,68},{5,69},{6,70},{7,71},{8,72},{9,... | collective-permute-start | bytes 1769480 | tf_op jit(solution)/shard_map/ppermute | solution.py:404
  137.6 18.1 %collective-permute-start.11 = (f32[1152,128]{1,0:T(8,128)S(1)}, f32[1152,128]{1,0:T(8,128)S(1)}, u32[]{:S(2)}, u32[]{:S(2)}) collective-permute-start(f32[1152,128]{1,0:T(8,128)S(1)} %stage0.3), channel_id=1, source_target_pairs={{0,192},{1,193},{2,194},{3,195},{4,196},{5,197},{6,198},{7,199},{8... | collective-permute-start | bytes 1769480 | tf_op jit(solution)/shard_map/ppermute | solution.py:404
  142.5 19.2 %collective-permute-start.12 = (f32[576,1152]{1,0:T(8,128)S(1)}, f32[576,1152]{1,0:T(8,128)S(1)}, u32[]{:S(2)}, u32[]{:S(2)}) collective-permute-start(f32[576,1152]{1,0:T(8,128)S(1)} %order.3.own_ref), channel_id=1, source_target_pairs={{0,32},{32,0},{1,33},{33,1},{2,34},{34,2},{3,35},{35,3},{4,36},{36... | collective-permute-start | bytes 7962632 | tf_op jit(solution)/shard_map/ppermute | solution.py:363
  142.6 20.6 %collective-permute-start.13 = (f32[1152,128]{1,0:T(8,128)S(1)}, f32[1152,128]{1,0:T(8,128)S(1)}, u32[]{:S(2)}, u32[]{:S(2)}) collective-permute-start(f32[1152,128]{1,0:T(8,128)S(1)} %collective-permute-done.8.refs_4_), channel_id=1, source_target_pairs={{192,128},{193,129},{194,130},{195,131},{196,132},{197,133},{198,1... | collective-permute-start | bytes 1769480 | tf_op jit(solution)/shard_map/ppermute | solution.py:404
  149.9 14.6 %collective-permute-start.14 = (f32[1152,128]{1,0:T(8,128)S(1)}, f32[1152,128]{1,0:T(8,128)S(1)}, u32[]{:S(2)}, u32[]{:S(2)}) collective-permute-start(f32[1152,128]{1,0:T(8,128)S(1)} %get-tuple-element.30), channel_id=1, source_target_pairs={{64,0},{65,1},{66,2},{67,3},{68,4},{69,5},{70,6},{71,7},{72,8},{73... | collective-permute-start | bytes 1769480 | tf_op jit(solution)/shard_map/ppermute | solution.py:404
  150.6 13.9 %collective-permute-start.15 = (f32[1152,128]{1,0:T(8,128)S(1)}, f32[1152,128]{1,0:T(8,128)S(1)}, u32[]{:S(2)}, u32[]{:S(2)}) collective-permute-start(f32[1152,128]{1,0:T(8,128)S(1)} %get-tuple-element.30), channel_id=1, source_target_pairs={{64,128},{65,129},{66,130},{67,131},{68,132},{69,133},{70,134},{71... | collective-permute-start | bytes 1769480 | tf_op jit(solution)/shard_map/ppermute | solution.py:404
  159.6 7.6 %collective-permute-start.19 = (f32[1152,128]{1,0:T(8,128)S(1)}, f32[1152,128]{1,0:T(8,128)S(1)}, u32[]{:S(2)}, u32[]{:S(2)}) collective-permute-start(f32[1152,128]{1,0:T(8,128)S(1)} %get-tuple-element.34), channel_id=1, source_target_pairs={{64,0},{65,1},{66,2},{67,3},{68,4},{69,5},{70,6},{71,7},{72,8},{73... | collective-permute-start | bytes 1769480 | tf_op jit(solution)/shard_map/ppermute | solution.py:404
  163.1 13.5 %collective-permute-start.18 = (f32[1152,128]{1,0:T(8,128)S(1)}, f32[1152,128]{1,0:T(8,128)S(1)}, u32[]{:S(2)}, u32[]{:S(2)}) collective-permute-start(f32[1152,128]{1,0:T(8,128)S(1)} %collective-permute-done.11.refs_4_), channel_id=1, source_target_pairs={{192,128},{193,129},{194,130},{195,131},{196,132},{197,133},{198,1... | collective-permute-start | bytes 1769480 | tf_op jit(solution)/shard_map/ppermute | solution.py:404
  164.5 18.5 %collective-permute-start.16 = (f32[1152,128]{1,0:T(8,128)S(1)}, f32[1152,128]{1,0:T(8,128)S(1)}, u32[]{:S(2)}, u32[]{:S(2)}) collective-permute-start(f32[1152,128]{1,0:T(8,128)S(1)} %stage2.2), channel_id=1, source_target_pairs={{0,192},{1,193},{2,194},{3,195},{4,196},{5,197},{6,198},{7,199},{8... | collective-permute-start | bytes 1769480 | tf_op jit(solution)/shard_map/ppermute | solution.py:404
  165.8 23.0 %collective-permute-start.17 = (f32[1152,128]{1,0:T(8,128)S(1)}, f32[1152,128]{1,0:T(8,128)S(1)}, u32[]{:S(2)}, u32[]{:S(2)}) collective-permute-start(f32[1152,128]{1,0:T(8,128)S(1)} %stage2.2), channel_id=1, source_target_pairs={{128,192},{129,193},{130,194},{131,195},{132,196},{133,197},{134,1... | collective-permute-start | bytes 1769480 | tf_op jit(solution)/shard_map/ppermute | solution.py:404
  176.6 19.8 %collective-permute-start.21 = (f32[1152,128]{1,0:T(8,128)S(1)}, f32[1152,128]{1,0:T(8,128)S(1)}, u32[]{:S(2)}, u32[]{:S(2)}) collective-permute-start(f32[1152,128]{1,0:T(8,128)S(1)} %stage2.3), channel_id=1, source_target_pairs={{0,192},{1,193},{2,194},{3,195},{4,196},{5,197},{6,198},{7,199},{8... | collective-permute-start | bytes 1769480 | tf_op jit(solution)/shard_map/ppermute | solution.py:404
  178.1 24.5 %collective-permute-start.22 = (f32[1152,128]{1,0:T(8,128)S(1)}, f32[1152,128]{1,0:T(8,128)S(1)}, u32[]{:S(2)}, u32[]{:S(2)}) collective-permute-start(f32[1152,128]{1,0:T(8,128)S(1)} %stage2.3), channel_id=1, source_target_pairs={{128,192},{129,193},{130,194},{131,195},{132,196},{133,197},{134,1... | collective-permute-start | bytes 1769480 | tf_op jit(solution)/shard_map/ppermute | solution.py:404
  (24 other events, 157.1 us)
Sparse Core Ops, SparseCore 0:
  26.7 92.4 all-gather.1

commit v4 on v3

--- a/solution.py
+++ b/solution.py
@@ -10,10 +10,6 @@
 LANES = 128
 
 
-def full_dot(left, right):
-    return jnp.dot(left, right, precision=HI, preferred_element_type=jnp.float32)
-
-
 def halves(value):
     high = value.astype(jnp.bfloat16)
     return high, (value - high.astype(jnp.float32)).astype(jnp.bfloat16)
@@ -30,6 +26,10 @@
     dot = functools.partial(jnp.dot, preferred_element_type=jnp.float32)
     wide = dot(lh, both)
     return wide[:, :LANES] + (wide[:, LANES:] + dot(ll, rh))
+
+
+def full_dot(left, right):
+    return three_dot(halves(left), split_right(right))
 
 
 def invert_kernel(rows, groups, pieces, tiles, x_ref, own_ref, left_ref, far0_ref, far1_ref, right_ref, o_ref, a_ref, m_ref):
@@ -97,19 +97,20 @@
         o_ref[:, tile * LANES : (tile + 1) * LANES] = a_ref[tile, :rows, :]
 
 
-def order_kernel(rows, pieces, pad_rows, tiles, whole_ref, o_ref, s_ref):
+def order_kernel(rows, pieces, pad_rows, tiles, whole_ref, *refs):
     per = rows // pieces
-    whole_ref = whole_ref.reshape(pieces * pad_rows, LANES)
-    for tile in range(tiles):
-
-        def move(row, carry):
-            s_ref[pl.ds(row, pieces, stride=per), :] = whole_ref[
-                pl.ds(row * tiles + tile, pieces, stride=pad_rows), :
-            ]
-            return carry
-
-        lax.fori_loop(0, per, move, 0, unroll=6)
-        o_ref[:, tile * LANES : (tile + 1) * LANES] = s_ref[...]
+    outs, s_ref = refs[:-1], refs[-1]
+    for block, out in enumerate(outs):
+        for tile in range(tiles):
+
+            def move(row, carry, block=block, tile=tile):
+                s_ref[pl.ds(row, pieces, stride=per), :] = whole_ref[
+                    pl.ds(block * pad_rows + row * tiles + tile, pieces, stride=len(outs) * pad_rows), :
+                ]
+                return carry
+
+            lax.fori_loop(0, per, move, 0, unroll=6)
+            out[:, tile * LANES : (tile + 1) * LANES] = s_ref[...]
 
 
 def pack_kernel(core_ref, own_ref, other_ref, o_ref):
@@ -371,19 +372,17 @@
             name="pack",
         )(core_arg + zero, own, other)
 
-    def ordered(which, whole, zero):
-        own = pl.pallas_call(
+    def ordered(whole):
+        return pl.pallas_call(
             functools.partial(order_kernel, rows, pieces, lpad, ltiles),
-            out_shape=jax.ShapeDtypeStruct((rows, span), jnp.float32),
-            grid=(1,),
-            in_specs=[pl.BlockSpec((pieces, 1, lpad, LANES), lambda i: (0, which, 0, 0), pipeline_mode=pl.Buffered(1))],
-            out_specs=here,
+            out_shape=(jax.ShapeDtypeStruct((rows, span), jnp.float32),) * 2,
+            in_specs=[here],
+            out_specs=(here, here),
             scratch_shapes=[pltpu.VMEM((rows, LANES), jnp.float32)],
             compiler_params=small,
-            cost_estimate=pl.CostEstimate(flops=1_000_000, bytes_accessed=8_000_000, transcendentals=0),
+            cost_estimate=pl.CostEstimate(flops=1_000_000, bytes_accessed=16_000_000, transcendentals=0),
             name="order",
-        )(whole.reshape(pieces, 2, lpad, LANES))
-        return paired(own, zero)
+        )(whole)
 
     block = jax.ShapeDtypeStruct((span, LANES), jnp.float32)
 
@@ -410,7 +409,8 @@
     whole, *first, x0s[-1] = lax.optimization_barrier((whole, *firsts[0], x0s[-1]))
     firsts[0] = tuple(first)
     firsts[-1] = send(x0s[-1], [(0, 1)]), send(x0s[-1], [(0, 3)])
-    a_mat = ordered(0, whole, 0)
+    own_a, own_b = ordered(whole)
+    a_mat = paired(own_a, 0)
     x1s, nexts, tokens = [], [], []
     for index, (state, (to1, to3)) in enumerate(zip(list(states), firsts)):
         if index > 0:
@@ -422,7 +422,7 @@
         x1s.append((x1, to2))
         nexts.append((near_x, to0))
     _, zero = after(core_arg, [x1 for x1, _ in x1s] + tokens)
-    b_mat = ordered(1, whole, zero)
+    b_mat = paired(own_b, zero)
     for state, x0, (x1, to2), (near_x, to0) in zip(states, x0s, x1s, nexts):
         (x2,) = stage(2, inverse, a_mat, b_mat, state, to2, to0, near_x)
         part = send(x2, [(0, 3)])

time: 221 us -> 220 us (level)
  waiting for transfers between devices: 102 us -> 106 us
  Pallas kernels: 37.4 us -> 34.7 us
    pallas_call x1, Pallas kernels: 10.6 us -> 7.78 us  [per_device(): pl.pallas_call(functools.partial(invert_kernel, rows, xs, zs, tiles), out...]
    ppermute x14, waiting for transfers between devices: 46.6 us -> 48.9 us  [send(): return lax.ppermute(value, 'y', pairs)]
    unnamed x42 -> x44, local copies, waits for them, and re-layouts: 8.58 us -> 7.49 us
  transfers between devices with their start and end apart: 27 -> 27, of which waited for: 13 -> 14; matrix products, arithmetic and copies ran while one was open for 4% -> 4% of each run, Pallas kernels for 13% -> 12%
where the time goes in v4:
time: 220 us
  waiting for transfers between devices  106 us (48%)
  starting transfers between devices  44.5 us (20%)
  Pallas kernels  34.7 us (16%)
  between operations  15.4 us (7%)
  local copies, waits for them, and re-layouts  14.6 us (7%)
  matrix products  2.6 us (1%)
  other arithmetic  2.37 us (1%)
    ppermute x14, waiting for transfers between devices, send(): return lax.ppermute(value, 'y', pairs)  48.9 us
    ppermute x1, waiting for transfers between devices, per_device(): lax.ppermute(near, 'x', ahead)  23.1 us
    pallas_call x8, Pallas kernels, stage(): pl.pallas_call(functools.partial(stage_kernel, rows, number), out_shape=(...  16.1 us
    all_to_all x1, waiting for transfers between devices, spread(): lax.all_to_all(copies, 'z', 0, 0, tiled=True)  15.6 us
    ppermute x14, starting transfers between devices, send(): return lax.ppermute(value, 'y', pairs)  15 us
    ppermute x1, waiting for transfers between devices, far(): lax.ppermute(left[:middle], 'x', ahead)  9.29 us
    all_to_all x1, starting transfers between devices, spread(): lax.all_to_all(copies, 'z', 0, 0, tiled=True)  8.19 us
    pallas_call x1, Pallas kernels, per_device(): pl.pallas_call(functools.partial(invert_kernel, rows, xs, zs, tiles), out...  7.78 us
  transfers between devices with their start and end apart: 27, of which 14 were waited for; matrix products, arithmetic and copies ran while one was open for 4% of the time, Pallas kernels for 12%

profile of v4, /device:TPU:31, one launch (start us, length us, event | category | flops | bytes accessed | tf_op | source)
XLA Modules:
  0.0 219.7 jit_solution(11055124372615750356)
XLA Ops:
  7.5 2.6 %collective-permute-start = (f32[18,288]{1,0:T(8,128)S(1)}, f32[18,288]{1,0:T(8,128)S(1)}, u32[]{:S(2)}, u32[]{:S(2)}) collective-permute-start(f32[18,288]{1,0:T(8,128)S(1)} %get-tuple-element.48), channel_id=1, source_target_pairs={{32,0},{33,1},{34,2},{35,3},{36,4},{37,5},{38,6},{39,7},{40,8},{41... | collective-permute-start | bytes 62216 | tf_op jit(solution)/shard_map/ppermute | solution.py:299
  15.1 8.2 %all-to-all-start = ((f32[8,144,128]{2,1,0:T(8,128)}), f32[8,144,128]{2,1,0:T(8,128)S(1)}, u32[]{:S(2)}, u32[]{:S(2)}) async-start(f32[8,144,128]{2,1,0:T(8,128)} %broadcast_in_dim.8), calls=%async_computation | async-start | bytes 1179648 | tf_op jit(solution)/shard_map/all_to_all | solution.py:309
  24.6 2.6 %convolution_bitcast_fusion = f32[64,8,576]{2,1,0:T(8,128)} fusion(f32[576,512]{1,0:T(8,128)S(1)} %copy-done, s32[512]{0:T(512)S(1)} %add.51), kind=kOutput, calls=%fused_computation | convolution fusion | flops 1812201472 | bytes 2361344 | tf_op jit(solution)/shard_map/dot_general | solution.py:277
  27.2 15.6 %all-to-all-done = f32[8,144,128]{2,1,0:T(8,128)S(1)} async-done(((f32[8,144,128]{2,1,0:T(8,128)}), f32[8,144,128]{2,1,0:T(8,128)S(1)}, u32[]{:S(2)}, u32[]{:S(2)}) %all-to-all-start) | async-done | bytes 589856 | tf_op jit(solution)/shard_map/all_to_all | solution.py:309
  42.7 5.6 %all-to-all-start.1 = ((f32[64,8,576]{2,1,0:T(8,128)}), f32[64,8,576]{2,1,0:T(8,128)S(1)}, u32[]{:S(2)}, u32[]{:S(2)}) async-start(f32[64,8,576]{2,1,0:T(8,128)} %convolution_bitcast_fusion), calls=%async_computation.1 | async-start | bytes 2621440 | tf_op jit(solution)/shard_map/all_to_all | solution.py:311
  49.9 23.1 %collective-permute-done.1.left_ref = f32[1152,128]{1,0:T(8,128)S(1)} collective-permute-done((f32[1152,128]{1,0:T(8,128)S(1)}, f32[1152,128]{1,0:T(8,128)S(1)}, u32[]{:S(2)}, u32[]{:S(2)}) %collective-permute-start.1) | collective-permute-done | bytes 589856 | tf_op jit(solution)/shard_map/ppermute | solution.py:318
  73.8 2.4 %collective-permute-start.2 = (f32[576,128]{1,0:T(8,128)}, f32[576,128]{1,0:T(8,128)S(1)}, u32[]{:S(2)}, u32[]{:S(2)}) collective-permute-start(f32[576,128]{1,0:T(8,128)} %slice.60), channel_id=1, source_target_pairs={{0,8},{8,16},{16,24},{24,0},{1,9},{9,17},{17,25},{25,1},{2,10},{10... | collective-permute-start | bytes 884744 | tf_op jit(solution)/shard_map/ppermute | solution.py:321
  77.2 9.3 %collective-permute-done.2.far0_ref = f32[576,128]{1,0:T(8,128)S(1)} collective-permute-done((f32[576,128]{1,0:T(8,128)}, f32[576,128]{1,0:T(8,128)S(1)}, u32[]{:S(2)}, u32[]{:S(2)}) %collective-permute-start.2) | collective-permute-done | bytes 294944 | tf_op jit(solution)/shard_map/ppermute | solution.py:321
  86.5 4.1 %collective-permute-done.4.far1_ref = f32[576,128]{1,0:T(8,128)} collective-permute-done((f32[576,128]{1,0:T(8,128)}, f32[576,128]{1,0:T(8,128)}, u32[]{:S(2)}, u32[]{:S(2)}) %collective-permute-start.4) | collective-permute-done | bytes 294944 | tf_op jit(solution)/shard_map/ppermute | solution.py:321
  92.7 7.8 %invert.1.own_ref = f32[576,1024]{1,0:T(8,128)S(1)} custom-call(s32[1]{0:T(128)} %bitcast.2.x_ref, f32[1152,128]{1,0:T(8,128)S(1)} %bitcast.23, f32[1152,128]{1,0:T(8,128)S(1)} %copy-done.6, f32[576,128]{1,0:T(8,128)S(1)} %collective-permute-done.2.far0_ref, f32[576,128]{1,0:T(8,128)} %collective-permute-done.4.far1_ref, f32[1152,128]{1,0:T(8,128)S(1)} %copy-done.8), custom_call_target="tpu_custom_call" | custom-call | flops 1000 | bytes 1000 | tf_op jit(solution)/shard_map/invert/pallas_call | solution.py:336
  100.5 3.9 %collective-permute-start.5 = (f32[576,1024]{1,0:T(8,128)S(1)}, f32[576,1024]{1,0:T(8,128)S(1)}, u32[]{:S(2)}, u32[]{:S(2)}) collective-permute-start(f32[576,1024]{1,0:T(8,128)S(1)} %invert.1.own_ref), channel_id=1, source_target_pairs={{0,32},{32,0},{1,33},{33,1},{2,34},{34,2},{3,35},{35,3},{4,36},{36... | collective-permute-start | bytes 7077896 | tf_op jit(solution)/shard_map/ppermute | solution.py:346
  112.5 15.2 %collective-permute-done.8.refs_4_ = f32[1152,128]{1,0:T(8,128)S(1)} collective-permute-done((f32[1152,128]{1,0:T(8,128)S(1)}, f32[1152,128]{1,0:T(8,128)S(1)}, u32[]{:S(2)}, u32[]{:S(2)}) %collective-permute-start.8) | collective-permute-done | bytes 589856 | tf_op jit(solution)/shard_map/ppermute | solution.py:403
  127.7 2.6 %copy-done.1 = f32[10752,128]{1,0:T(8,128)S(1)} copy-done((f32[10752,128]{1,0:T(8,128)S(1)}, f32[10752,128]{1,0:T(8,128)}, u32[]{:S(2)}) %copy-start.1) | copy-done | bytes 5505048
  130.3 3.8 %order.1 = (f32[576,1152]{1,0:T(8,128)}, f32[576,1152]{1,0:T(8,128)S(1)}) custom-call(f32[10752,128]{1,0:T(8,128)S(1)} %copy-done.1), custom_call_target="tpu_custom_call" | custom-call | flops 1000000 | bytes 16000000 | tf_op jit(solution)/shard_map/order/pallas_call | solution.py:376
  141.6 3.3 %pack.4.refs_1_ = bf16[2,2,576,1152]{3,2,1,0:T(8,128)(2,1)S(1)} custom-call(s32[1]{0:T(128)} %bitcast.1.core_ref, f32[576,1152]{1,0:T(8,128)} %get-tuple-element.30.own_ref, f32[576,1152]{1,0:T(8,128)} %collective-permute-done.9.other_ref), custom_call_target="tpu_custom_call" | custom-call | flops 1000000 | bytes 8000000 | tf_op jit(solution)/shard_map/pack/pallas_call | solution.py:365
  145.0 2.5 %stage1.2 = (f32[1152,128]{1,0:T(8,128)S(1)}, f32[1152,128]{1,0:T(8,128)S(1)}) custom-call(s32[1]{0:T(128)} %bitcast.plane_ref, bf16[2,2,576,1024]{3,2,1,0:T(8,128)(2,1)S(1)} %bitcast.20, bf16[2,2,576,1152]{3,2,1,0:T(8,128)(2,1)S(1)} %pack.4.refs_1_, f32[1152,128]{1,0:T(8,128)S(1)} %copy-done.14, f32[1152,128]{1,0:T(8,128)S(1)} %copy-done.16, ...), custom_call_target="tpu_custom_call" | custom-call | flops 30000001024 | bytes 4000000 | tf_op jit(solution)/shard_map/stage1/pallas_call | solution.py:391
  148.9 6.6 %collective-permute-done.11.refs_4_ = f32[1152,128]{1,0:T(8,128)S(1)} collective-permute-done((f32[1152,128]{1,0:T(8,128)S(1)}, f32[1152,128]{1,0:T(8,128)S(1)}, u32[]{:S(2)}, u32[]{:S(2)}) %collective-permute-start.11) | collective-permute-done | bytes 589856 | tf_op jit(solution)/shard_map/ppermute | solution.py:403
  155.5 2.7 %stage1.3 = (f32[1152,128]{1,0:T(8,128)S(1)}, f32[1152,128]{1,0:T(8,128)S(1)}) custom-call(s32[1]{0:T(128)} %bitcast.plane_ref, bf16[2,2,576,1024]{3,2,1,0:T(8,128)(2,1)S(1)} %bitcast.20, bf16[2,2,576,1152]{3,2,1,0:T(8,128)(2,1)S(1)} %pack.4.refs_1_, f32[1152,128]{1,0:T(8,128)S(1)} %get-tuple-element.28.refs_1_.refs_2_, ...), custom_call_target="tpu_custom_call" | custom-call | flops 30000001024 | bytes 4000000 | tf_op jit(solution)/shard_map/stage1/pallas_call | solution.py:391
  166.9 9.4 %collective-permute-done.18.refs_4_ = f32[1152,128]{1,0:T(8,128)S(1)} collective-permute-done((f32[1152,128]{1,0:T(8,128)S(1)}, f32[1152,128]{1,0:T(8,128)S(1)}, u32[]{:S(2)}, u32[]{:S(2)}) %collective-permute-start.18) | collective-permute-done | bytes 589856 | tf_op jit(solution)/shard_map/ppermute | solution.py:403
  179.1 2.5 %collective-permute-done.16.refs_3_ = f32[1152,128]{1,0:T(8,128)S(1)} collective-permute-done((f32[1152,128]{1,0:T(8,128)S(1)}, f32[1152,128]{1,0:T(8,128)S(1)}, u32[]{:S(2)}, u32[]{:S(2)}) %collective-permute-start.16) | collective-permute-done | bytes 589856 | tf_op jit(solution)/shard_map/ppermute | solution.py:403
  181.6 7.0 %collective-permute-done.17.refs_4_ = f32[1152,128]{1,0:T(8,128)S(1)} collective-permute-done((f32[1152,128]{1,0:T(8,128)S(1)}, f32[1152,128]{1,0:T(8,128)S(1)}, u32[]{:S(2)}, u32[]{:S(2)}) %collective-permute-start.17) | collective-permute-done | bytes 589856 | tf_op jit(solution)/shard_map/ppermute | solution.py:403
  188.6 5.3 %stage3.2 = f32[1152,128]{1,0:T(8,128)S(1)} custom-call(s32[1]{0:T(128)} %bitcast.plane_ref, bf16[2,2,576,1024]{3,2,1,0:T(8,128)(2,1)S(1)} %bitcast.20, bf16[2,2,576,1152]{3,2,1,0:T(8,128)(2,1)S(1)} %pack.5.refs_2_.refs_1_, f32[1152,128]{1,0:T(8,128)S(1)} %get-tuple-element.41.refs_3_.refs_2_, f32[1152,128]{1,0:T(8,128)S(1)} %collective-permute-done.16.refs_3_, ...), custom_call_target="tpu_custom_call" | custom-call | flops 30000001024 | bytes 4000000 | tf_op jit(solution)/shard_map/stage3/pallas_call | solution.py:391
  194.9 7.5 %collective-permute-done.22.refs_4_ = f32[1152,128]{1,0:T(8,128)S(1)} collective-permute-done((f32[1152,128]{1,0:T(8,128)S(1)}, f32[1152,128]{1,0:T(8,128)S(1)}, u32[]{:S(2)}, u32[]{:S(2)}) %collective-permute-start.22) | collective-permute-done | bytes 589856 | tf_op jit(solution)/shard_map/ppermute | solution.py:403
  202.4 5.4 %stage3.3 = f32[1152,128]{1,0:T(8,128)S(1)} custom-call(s32[1]{0:T(128)} %bitcast.plane_ref, bf16[2,2,576,1024]{3,2,1,0:T(8,128)(2,1)S(1)} %bitcast.20, bf16[2,2,576,1152]{3,2,1,0:T(8,128)(2,1)S(1)} %pack.5.refs_2_.refs_1_, f32[1152,128]{1,0:T(8,128)S(1)} %get-tuple-element.42.refs_3_.refs_2_, f32[1152,128]{1,0:T(8,128)S(1)} %collective-permute-done.21.refs_3_, ...), custom_call_target="tpu_custom_call" | custom-call | flops 30000001024 | bytes 4000000 | tf_op jit(solution)/shard_map/stage3/pallas_call | solution.py:391
  (121 shorter events, 45.6 us)
Async XLA Ops:
  7.5 6.6 %collective-permute-start = (f32[18,288]{1,0:T(8,128)S(1)}, f32[18,288]{1,0:T(8,128)S(1)}, u32[]{:S(2)}, u32[]{:S(2)}) collective-permute-start(f32[18,288]{1,0:T(8,128)S(1)} %get-tuple-element.48), channel_id=1, source_target_pairs={{32,0},{33,1},{34,2},{35,3},{36,4},{37,5},{38,6},{39,7},{40,8},{41... | collective-permute-start | bytes 62216 | tf_op jit(solution)/shard_map/ppermute | solution.py:299
  11.0 12.6 %collective-permute-start.6 = (f32[18,1152]{1,0:T(8,128)S(1)}, f32[18,1152]{1,0:T(8,128)S(1)}, u32[]{:S(2)}, u32[]{:S(2)}) collective-permute-start(f32[18,1152]{1,0:T(8,128)S(1)} %slice.52), channel_id=1, source_target_pairs={{192,0},{193,1},{194,2},{195,3},{196,4},{197,5},{198,6},{199,7},{2... | collective-permute-start | bytes 248840 | tf_op jit(solution)/shard_map/ppermute | solution.py:285
  15.1 27.7 %all-to-all-start = ((f32[8,144,128]{2,1,0:T(8,128)}), f32[8,144,128]{2,1,0:T(8,128)S(1)}, u32[]{:S(2)}, u32[]{:S(2)}) async-start(f32[8,144,128]{2,1,0:T(8,128)} %broadcast_in_dim.8), calls=%async_computation | async-start | bytes 1179648 | tf_op jit(solution)/shard_map/all_to_all | solution.py:309
  23.3 104.5 %all-gather.2.cloned.1.call-start = ((), (), s32[]{:S(2)}) async-start(), calls=%async_computation.2 | async-start | bytes 5677056 | tf_op jit(solution)/shard_map/all_gather | solution.py:313
  42.7 47.9 %all-to-all-start.1 = ((f32[64,8,576]{2,1,0:T(8,128)}), f32[64,8,576]{2,1,0:T(8,128)S(1)}, u32[]{:S(2)}, u32[]{:S(2)}) async-start(f32[64,8,576]{2,1,0:T(8,128)} %convolution_bitcast_fusion), calls=%async_computation.1 | async-start | bytes 2621440 | tf_op jit(solution)/shard_map/all_to_all | solution.py:311
  48.4 24.6 %collective-permute-start.1 = (f32[1152,128]{1,0:T(8,128)S(1)}, f32[1152,128]{1,0:T(8,128)S(1)}, u32[]{:S(2)}, u32[]{:S(2)}) collective-permute-start(f32[1152,128]{1,0:T(8,128)S(1)} %bitcast.21), channel_id=1, source_target_pairs={{0,8},{8,16},{16,24},{24,0},{1,9},{9,17},{17,25},{25,1},{2,10},{10... | collective-permute-start | bytes 1769480 | tf_op jit(solution)/shard_map/ppermute | solution.py:318
  48.5 27.8 %collective-permute-start.3 = (f32[1152,128]{1,0:T(8,128)S(1)}, f32[1152,128]{1,0:T(8,128)S(1)}, u32[]{:S(2)}, u32[]{:S(2)}) collective-permute-start(f32[1152,128]{1,0:T(8,128)S(1)} %bitcast.22), channel_id=1, source_target_pairs={{0,24},{8,0},{16,8},{24,16},{1,25},{9,1},{17,9},{25,17},{2,26},{10... | collective-permute-start | bytes 1769480 | tf_op jit(solution)/shard_map/ppermute | solution.py:318
  73.8 12.7 %collective-permute-start.2 = (f32[576,128]{1,0:T(8,128)}, f32[576,128]{1,0:T(8,128)S(1)}, u32[]{:S(2)}, u32[]{:S(2)}) collective-permute-start(f32[576,128]{1,0:T(8,128)} %slice.60), channel_id=1, source_target_pairs={{0,8},{8,16},{16,24},{24,0},{1,9},{9,17},{17,25},{25,1},{2,10},{10... | collective-permute-start | bytes 884744 | tf_op jit(solution)/shard_map/ppermute | solution.py:321
  77.2 13.4 %collective-permute-start.4 = (f32[576,128]{1,0:T(8,128)}, f32[576,128]{1,0:T(8,128)}, u32[]{:S(2)}, u32[]{:S(2)}) collective-permute-start(f32[576,128]{1,0:T(8,128)} %slice.61), channel_id=1, source_target_pairs={{0,24},{8,0},{16,8},{24,16},{1,25},{9,1},{17,9},{25,17},{2,26},{10... | collective-permute-start | bytes 884744 | tf_op jit(solution)/shard_map/ppermute | solution.py:321
  100.5 8.0 %collective-permute-start.5 = (f32[576,1024]{1,0:T(8,128)S(1)}, f32[576,1024]{1,0:T(8,128)S(1)}, u32[]{:S(2)}, u32[]{:S(2)}) collective-permute-start(f32[576,1024]{1,0:T(8,128)S(1)} %invert.1.own_ref), channel_id=1, source_target_pairs={{0,32},{32,0},{1,33},{33,1},{2,34},{34,2},{3,35},{35,3},{4,36},{36... | collective-permute-start | bytes 7077896 | tf_op jit(solution)/shard_map/ppermute | solution.py:346
  110.1 17.6 %collective-permute-start.8 = (f32[1152,128]{1,0:T(8,128)S(1)}, f32[1152,128]{1,0:T(8,128)S(1)}, u32[]{:S(2)}, u32[]{:S(2)}) collective-permute-start(f32[1152,128]{1,0:T(8,128)S(1)} %stage0.2), channel_id=1, source_target_pairs={{0,192},{1,193},{2,194},{3,195},{4,196},{5,197},{6,198},{7,199},{8... | collective-permute-start | bytes 1769480 | tf_op jit(solution)/shard_map/ppermute | solution.py:403
  135.5 6.1 %collective-permute-start.9 = (f32[576,1152]{1,0:T(8,128)}, f32[576,1152]{1,0:T(8,128)}, u32[]{:S(2)}, u32[]{:S(2)}) collective-permute-start(f32[576,1152]{1,0:T(8,128)} %get-tuple-element.30.own_ref), channel_id=1, source_target_pairs={{0,32},{32,0},{1,33},{33,1},{2,34},{34,2},{3,35},{35,3},{4,36},{36... | collective-permute-start | bytes 7962632 | tf_op jit(solution)/shard_map/ppermute | solution.py:364
  136.7 11.5 %collective-permute-start.10 = (f32[1152,128]{1,0:T(8,128)S(1)}, f32[1152,128]{1,0:T(8,128)S(1)}, u32[]{:S(2)}, u32[]{:S(2)}) collective-permute-start(f32[1152,128]{1,0:T(8,128)S(1)} %stage0.3), channel_id=1, source_target_pairs={{0,64},{1,65},{2,66},{3,67},{4,68},{5,69},{6,70},{7,71},{8,72},{9,... | collective-permute-start | bytes 1769480 | tf_op jit(solution)/shard_map/ppermute | solution.py:403
  137.4 18.1 %collective-permute-start.11 = (f32[1152,128]{1,0:T(8,128)S(1)}, f32[1152,128]{1,0:T(8,128)S(1)}, u32[]{:S(2)}, u32[]{:S(2)}) collective-permute-start(f32[1152,128]{1,0:T(8,128)S(1)} %stage0.3), channel_id=1, source_target_pairs={{0,192},{1,193},{2,194},{3,195},{4,196},{5,197},{6,198},{7,199},{8... | collective-permute-start | bytes 1769480 | tf_op jit(solution)/shard_map/ppermute | solution.py:403
  138.8 22.7 %collective-permute-start.12 = (f32[576,1152]{1,0:T(8,128)}, f32[576,1152]{1,0:T(8,128)S(1)}, u32[]{:S(2)}, u32[]{:S(2)}) collective-permute-start(f32[576,1152]{1,0:T(8,128)} %copy-done.3), channel_id=1, source_target_pairs={{0,32},{32,0},{1,33},{33,1},{2,34},{34,2},{3,35},{35,3},{4,36},{36... | collective-permute-start | bytes 7962632 | tf_op jit(solution)/shard_map/ppermute | solution.py:364
  138.9 24.0 %collective-permute-start.13 = (f32[1152,128]{1,0:T(8,128)S(1)}, f32[1152,128]{1,0:T(8,128)S(1)}, u32[]{:S(2)}, u32[]{:S(2)}) collective-permute-start(f32[1152,128]{1,0:T(8,128)S(1)} %collective-permute-done.8.refs_4_), channel_id=1, source_target_pairs={{192,128},{193,129},{194,130},{195,131},{196,132},{197,133},{198,1... | collective-permute-start | bytes 1769480 | tf_op jit(solution)/shard_map/ppermute | solution.py:403
  147.5 16.7 %collective-permute-start.14 = (f32[1152,128]{1,0:T(8,128)S(1)}, f32[1152,128]{1,0:T(8,128)S(1)}, u32[]{:S(2)}, u32[]{:S(2)}) collective-permute-start(f32[1152,128]{1,0:T(8,128)S(1)} %get-tuple-element.33), channel_id=1, source_target_pairs={{64,0},{65,1},{66,2},{67,3},{68,4},{69,5},{70,6},{71,7},{72,8},{73... | collective-permute-start | bytes 1769480 | tf_op jit(solution)/shard_map/ppermute | solution.py:403
  148.2 16.0 %collective-permute-start.15 = (f32[1152,128]{1,0:T(8,128)S(1)}, f32[1152,128]{1,0:T(8,128)S(1)}, u32[]{:S(2)}, u32[]{:S(2)}) collective-permute-start(f32[1152,128]{1,0:T(8,128)S(1)} %get-tuple-element.33), channel_id=1, source_target_pairs={{64,128},{65,129},{66,130},{67,131},{68,132},{69,133},{70,134},{71... | collective-permute-start | bytes 1769480 | tf_op jit(solution)/shard_map/ppermute | solution.py:403
  159.4 7.6 %collective-permute-start.19 = (f32[1152,128]{1,0:T(8,128)S(1)}, f32[1152,128]{1,0:T(8,128)S(1)}, u32[]{:S(2)}, u32[]{:S(2)}) collective-permute-start(f32[1152,128]{1,0:T(8,128)S(1)} %get-tuple-element.37), channel_id=1, source_target_pairs={{64,0},{65,1},{66,2},{67,3},{68,4},{69,5},{70,6},{71,7},{72,8},{73... | collective-permute-start | bytes 1769480 | tf_op jit(solution)/shard_map/ppermute | solution.py:403
  162.9 13.5 %collective-permute-start.18 = (f32[1152,128]{1,0:T(8,128)S(1)}, f32[1152,128]{1,0:T(8,128)S(1)}, u32[]{:S(2)}, u32[]{:S(2)}) collective-permute-start(f32[1152,128]{1,0:T(8,128)S(1)} %collective-permute-done.11.refs_4_), channel_id=1, source_target_pairs={{192,128},{193,129},{194,130},{195,131},{196,132},{197,133},{198,1... | collective-permute-start | bytes 1769480 | tf_op jit(solution)/shard_map/ppermute | solution.py:403
  164.3 17.3 %collective-permute-start.16 = (f32[1152,128]{1,0:T(8,128)S(1)}, f32[1152,128]{1,0:T(8,128)S(1)}, u32[]{:S(2)}, u32[]{:S(2)}) collective-permute-start(f32[1152,128]{1,0:T(8,128)S(1)} %stage2.2), channel_id=1, source_target_pairs={{0,192},{1,193},{2,194},{3,195},{4,196},{5,197},{6,198},{7,199},{8... | collective-permute-start | bytes 1769480 | tf_op jit(solution)/shard_map/ppermute | solution.py:403
  165.6 23.0 %collective-permute-start.17 = (f32[1152,128]{1,0:T(8,128)S(1)}, f32[1152,128]{1,0:T(8,128)S(1)}, u32[]{:S(2)}, u32[]{:S(2)}) collective-permute-start(f32[1152,128]{1,0:T(8,128)S(1)} %stage2.2), channel_id=1, source_target_pairs={{128,192},{129,193},{130,194},{131,195},{132,196},{133,197},{134,1... | collective-permute-start | bytes 1769480 | tf_op jit(solution)/shard_map/ppermute | solution.py:403
  176.4 18.5 %collective-permute-start.21 = (f32[1152,128]{1,0:T(8,128)S(1)}, f32[1152,128]{1,0:T(8,128)S(1)}, u32[]{:S(2)}, u32[]{:S(2)}) collective-permute-start(f32[1152,128]{1,0:T(8,128)S(1)} %stage2.3), channel_id=1, source_target_pairs={{0,192},{1,193},{2,194},{3,195},{4,196},{5,197},{6,198},{7,199},{8... | collective-permute-start | bytes 1769480 | tf_op jit(solution)/shard_map/ppermute | solution.py:403
  177.8 24.5 %collective-permute-start.22 = (f32[1152,128]{1,0:T(8,128)S(1)}, f32[1152,128]{1,0:T(8,128)S(1)}, u32[]{:S(2)}, u32[]{:S(2)}) collective-permute-start(f32[1152,128]{1,0:T(8,128)S(1)} %stage2.3), channel_id=1, source_target_pairs={{128,192},{129,193},{130,194},{131,195},{132,196},{133,197},{134,1... | collective-permute-start | bytes 1769480 | tf_op jit(solution)/shard_map/ppermute | solution.py:403
  (25 other events, 166.6 us)
Sparse Core Ops, SparseCore 0:
  26.7 92.4 all-gather.1

commit v5 on v4

--- a/solution.py
+++ b/solution.py
@@ -204,6 +204,14 @@
         to_ref[...] = second_ref[...]
 
 
+def early_kernel(plane_ref, a_ref, r_ref, seen_ref, out_ref):
+    out_ref[...] = r_ref[...]
+
+    @pl.when(plane_ref[0] == 2)
+    def _():
+        subtract(out_ref, a_ref, seen_ref)
+
+
 def stage_kernel(rows, number, plane_ref, *refs):
     plane = plane_ref[0]
     span = 2 * rows
@@ -229,7 +237,14 @@
                 def _():
                     state[...] = jnp.zeros_like(state)
 
-            subtract(state, a_ref, seen)
+            if number == 1:
+                subtract(state, a_ref, seen)
+            else:
+
+                @pl.when(plane == 0)
+                def _():
+                    subtract(state, a_ref, seen)
+
         if number == 3:
             state[0:span, :] = state[0:span, :] + arrived[0][...]
 
@@ -424,6 +439,15 @@
     _, zero = after(core_arg, [x1 for x1, _ in x1s] + tokens)
     b_mat = paired(own_b, zero)
     for state, x0, (x1, to2), (near_x, to0) in zip(states, x0s, x1s, nexts):
+        state = pl.pallas_call(
+            early_kernel,
+            out_shape=block,
+            in_specs=[smem, here, here, here],
+            out_specs=here,
+            compiler_params=small,
+            cost_estimate=cheap,
+            name="early",
+        )(plane_arg, a_mat, state, to2)
         (x2,) = stage(2, inverse, a_mat, b_mat, state, to2, to0, near_x)
         part = send(x2, [(0, 3)])
         near_x = send(x2, [(2, 3)])

time: 220 us -> 218 us (level)
  waiting for transfers between devices: 106 us -> 103 us
    ppermute x14, waiting for transfers between devices: 48.9 us -> 46.2 us  [send(): return lax.ppermute(value, 'y', pairs)]
where the time goes in v5:
time: 218 us; the launch traced here: 217 us
  waiting for transfers between devices  103 us (47%)
  starting transfers between devices  44.2 us (20%)
  Pallas kernels  35 us (16%)
  between operations  15.4 us (7%)
  local copies, waits for them, and re-layouts  14.6 us (7%)
  matrix products  2.6 us (1%)
  other arithmetic  2.22 us (1%)
    ppermute x14, waiting for transfers between devices, send(): return lax.ppermute(value, 'y', pairs)  46.2 us
    ppermute x1, waiting for transfers between devices, per_device(): lax.ppermute(near, 'x', ahead)  23.1 us
    pallas_call x8, Pallas kernels, stage(): pl.pallas_call(functools.partial(stage_kernel, rows, number), out_shape=(...  16.1 us
    all_to_all x1, waiting for transfers between devices, spread(): lax.all_to_all(copies, 'z', 0, 0, tiled=True)  15.6 us
    ppermute x14, starting transfers between devices, send(): return lax.ppermute(value, 'y', pairs)  14.7 us
    ppermute x1, waiting for transfers between devices, far(): lax.ppermute(left[:middle], 'x', ahead)  9.29 us
    all_to_all x1, starting transfers between devices, spread(): lax.all_to_all(copies, 'z', 0, 0, tiled=True)  8.19 us
    pallas_call x1, Pallas kernels, per_device(): pl.pallas_call(functools.partial(invert_kernel, rows, xs, zs, tiles), out...  7.78 us
  transfers between devices with their start and end apart: 27, of which 14 were waited for; matrix products, arithmetic and copies ran while one was open for 4% of the time, Pallas kernels for 12%

profile of v5, /device:TPU:31, one launch (start us, length us, event | category | flops | bytes accessed | tf_op | source)
XLA Modules:
  0.0 217.1 jit_solution(13748488703156658930)
XLA Ops:
  7.5 2.6 %collective-permute-start = (f32[18,288]{1,0:T(8,128)S(1)}, f32[18,288]{1,0:T(8,128)S(1)}, u32[]{:S(2)}, u32[]{:S(2)}) collective-permute-start(f32[18,288]{1,0:T(8,128)S(1)} %get-tuple-element.48), channel_id=1, source_target_pairs={{32,0},{33,1},{34,2},{35,3},{36,4},{37,5},{38,6},{39,7},{40,8},{41... | collective-permute-start | bytes 62216 | tf_op jit(solution)/shard_map/ppermute | solution.py:314
  15.1 8.2 %all-to-all-start = ((f32[8,144,128]{2,1,0:T(8,128)}), f32[8,144,128]{2,1,0:T(8,128)S(1)}, u32[]{:S(2)}, u32[]{:S(2)}) async-start(f32[8,144,128]{2,1,0:T(8,128)} %broadcast_in_dim.8), calls=%async_computation | async-start | bytes 1179648 | tf_op jit(solution)/shard_map/all_to_all | solution.py:324
  24.6 2.6 %convolution_bitcast_fusion = f32[64,8,576]{2,1,0:T(8,128)} fusion(f32[576,512]{1,0:T(8,128)S(1)} %copy-done, s32[512]{0:T(512)S(1)} %add.51), kind=kOutput, calls=%fused_computation | convolution fusion | flops 1812201472 | bytes 2361344 | tf_op jit(solution)/shard_map/dot_general | solution.py:292
  27.2 15.6 %all-to-all-done = f32[8,144,128]{2,1,0:T(8,128)S(1)} async-done(((f32[8,144,128]{2,1,0:T(8,128)}), f32[8,144,128]{2,1,0:T(8,128)S(1)}, u32[]{:S(2)}, u32[]{:S(2)}) %all-to-all-start) | async-done | bytes 589856 | tf_op jit(solution)/shard_map/all_to_all | solution.py:324
  42.7 5.6 %all-to-all-start.1 = ((f32[64,8,576]{2,1,0:T(8,128)}), f32[64,8,576]{2,1,0:T(8,128)S(1)}, u32[]{:S(2)}, u32[]{:S(2)}) async-start(f32[64,8,576]{2,1,0:T(8,128)} %convolution_bitcast_fusion), calls=%async_computation.1 | async-start | bytes 2621440 | tf_op jit(solution)/shard_map/all_to_all | solution.py:326
  49.9 23.1 %collective-permute-done.1.left_ref = f32[1152,128]{1,0:T(8,128)S(1)} collective-permute-done((f32[1152,128]{1,0:T(8,128)S(1)}, f32[1152,128]{1,0:T(8,128)S(1)}, u32[]{:S(2)}, u32[]{:S(2)}) %collective-permute-start.1) | collective-permute-done | bytes 589856 | tf_op jit(solution)/shard_map/ppermute | solution.py:333
  73.8 2.4 %collective-permute-start.2 = (f32[576,128]{1,0:T(8,128)}, f32[576,128]{1,0:T(8,128)S(1)}, u32[]{:S(2)}, u32[]{:S(2)}) collective-permute-start(f32[576,128]{1,0:T(8,128)} %slice.60), channel_id=1, source_target_pairs={{0,8},{8,16},{16,24},{24,0},{1,9},{9,17},{17,25},{25,1},{2,10},{10... | collective-permute-start | bytes 884744 | tf_op jit(solution)/shard_map/ppermute | solution.py:336
  77.2 9.3 %collective-permute-done.2.far0_ref = f32[576,128]{1,0:T(8,128)S(1)} collective-permute-done((f32[576,128]{1,0:T(8,128)}, f32[576,128]{1,0:T(8,128)S(1)}, u32[]{:S(2)}, u32[]{:S(2)}) %collective-permute-start.2) | collective-permute-done | bytes 294944 | tf_op jit(solution)/shard_map/ppermute | solution.py:336
  86.5 4.1 %collective-permute-done.4.far1_ref = f32[576,128]{1,0:T(8,128)} collective-permute-done((f32[576,128]{1,0:T(8,128)}, f32[576,128]{1,0:T(8,128)}, u32[]{:S(2)}, u32[]{:S(2)}) %collective-permute-start.4) | collective-permute-done | bytes 294944 | tf_op jit(solution)/shard_map/ppermute | solution.py:336
  92.7 7.8 %invert.1.own_ref = f32[576,1024]{1,0:T(8,128)S(1)} custom-call(s32[1]{0:T(128)} %bitcast.2.x_ref, f32[1152,128]{1,0:T(8,128)S(1)} %bitcast.23, f32[1152,128]{1,0:T(8,128)S(1)} %copy-done.6, f32[576,128]{1,0:T(8,128)S(1)} %collective-permute-done.2.far0_ref, f32[576,128]{1,0:T(8,128)} %collective-permute-done.4.far1_ref, f32[1152,128]{1,0:T(8,128)S(1)} %copy-done.8), custom_call_target="tpu_custom_call" | custom-call | flops 1000 | bytes 1000 | tf_op jit(solution)/shard_map/invert/pallas_call | solution.py:351
  100.5 3.9 %collective-permute-start.5 = (f32[576,1024]{1,0:T(8,128)S(1)}, f32[576,1024]{1,0:T(8,128)S(1)}, u32[]{:S(2)}, u32[]{:S(2)}) collective-permute-start(f32[576,1024]{1,0:T(8,128)S(1)} %invert.1.own_ref), channel_id=1, source_target_pairs={{0,32},{32,0},{1,33},{33,1},{2,34},{34,2},{3,35},{35,3},{4,36},{36... | collective-permute-start | bytes 7077896 | tf_op jit(solution)/shard_map/ppermute | solution.py:361
  112.5 15.2 %collective-permute-done.8.refs_4_ = f32[1152,128]{1,0:T(8,128)S(1)} collective-permute-done((f32[1152,128]{1,0:T(8,128)S(1)}, f32[1152,128]{1,0:T(8,128)S(1)}, u32[]{:S(2)}, u32[]{:S(2)}) %collective-permute-start.8) | collective-permute-done | bytes 589856 | tf_op jit(solution)/shard_map/ppermute | solution.py:418
  127.7 2.6 %copy-done.1 = f32[10752,128]{1,0:T(8,128)S(1)} copy-done((f32[10752,128]{1,0:T(8,128)S(1)}, f32[10752,128]{1,0:T(8,128)}, u32[]{:S(2)}) %copy-start.1) | copy-done | bytes 5505048
  130.2 3.8 %order.1 = (f32[576,1152]{1,0:T(8,128)}, f32[576,1152]{1,0:T(8,128)S(1)}) custom-call(f32[10752,128]{1,0:T(8,128)S(1)} %copy-done.1), custom_call_target="tpu_custom_call" | custom-call | flops 1000000 | bytes 16000000 | tf_op jit(solution)/shard_map/order/pallas_call | solution.py:391
  141.6 3.5 %pack.4.refs_1_.a_ref = bf16[2,2,576,1152]{3,2,1,0:T(8,128)(2,1)S(1)} custom-call(s32[1]{0:T(128)} %bitcast.1.core_ref, f32[576,1152]{1,0:T(8,128)} %get-tuple-element.30.own_ref, f32[576,1152]{1,0:T(8,128)} %collective-permute-done.9.other_ref), custom_call_target="tpu_custom_call" | custom-call | flops 1000000 | bytes 8000000 | tf_op jit(solution)/shard_map/pack/pallas_call | solution.py:380
  145.1 2.5 %stage1.2 = (f32[1152,128]{1,0:T(8,128)S(1)}, f32[1152,128]{1,0:T(8,128)S(1)}) custom-call(s32[1]{0:T(128)} %bitcast.plane_ref, bf16[2,2,576,1024]{3,2,1,0:T(8,128)(2,1)S(1)} %bitcast.20, bf16[2,2,576,1152]{3,2,1,0:T(8,128)(2,1)S(1)} %pack.4.refs_1_.a_ref, f32[1152,128]{1,0:T(8,128)S(1)} %copy-done.14, f32[1152,128]{1,0:T(8,128)S(1)} %copy-done.16, ...), custom_call_target="tpu_custom_call" | custom-call | flops 30000001024 | bytes 4000000 | tf_op jit(solution)/shard_map/stage1/pallas_call | solution.py:406
  149.0 6.4 %collective-permute-done.11.refs_4_ = f32[1152,128]{1,0:T(8,128)S(1)} collective-permute-done((f32[1152,128]{1,0:T(8,128)S(1)}, f32[1152,128]{1,0:T(8,128)S(1)}, u32[]{:S(2)}, u32[]{:S(2)}) %collective-permute-start.11) | collective-permute-done | bytes 589856 | tf_op jit(solution)/shard_map/ppermute | solution.py:418
  156.8 2.7 %stage1.3 = (f32[1152,128]{1,0:T(8,128)S(1)}, f32[1152,128]{1,0:T(8,128)S(1)}) custom-call(s32[1]{0:T(128)} %bitcast.plane_ref, bf16[2,2,576,1024]{3,2,1,0:T(8,128)(2,1)S(1)} %bitcast.20, bf16[2,2,576,1152]{3,2,1,0:T(8,128)(2,1)S(1)} %pack.4.refs_1_.a_ref, f32[1152,128]{1,0:T(8,128)S(1)} %get-tuple-element.28.refs_1_.refs_2_, ...), custom_call_target="tpu_custom_call" | custom-call | flops 30000001024 | bytes 4000000 | tf_op jit(solution)/shard_map/stage1/pallas_call | solution.py:406
  171.8 9.6 %collective-permute-done.16.refs_3_ = f32[1152,128]{1,0:T(8,128)S(1)} collective-permute-done((f32[1152,128]{1,0:T(8,128)S(1)}, f32[1152,128]{1,0:T(8,128)S(1)}, u32[]{:S(2)}, u32[]{:S(2)}) %collective-permute-start.16) | collective-permute-done | bytes 589856 | tf_op jit(solution)/shard_map/ppermute | solution.py:418
  181.4 4.8 %collective-permute-done.17.refs_4_ = f32[1152,128]{1,0:T(8,128)S(1)} collective-permute-done((f32[1152,128]{1,0:T(8,128)S(1)}, f32[1152,128]{1,0:T(8,128)S(1)}, u32[]{:S(2)}, u32[]{:S(2)}) %collective-permute-start.17) | collective-permute-done | bytes 589856 | tf_op jit(solution)/shard_map/ppermute | solution.py:418
  186.2 5.3 %stage3.2 = f32[1152,128]{1,0:T(8,128)S(1)} custom-call(s32[1]{0:T(128)} %bitcast.plane_ref, bf16[2,2,576,1024]{3,2,1,0:T(8,128)(2,1)S(1)} %bitcast.20, bf16[2,2,576,1152]{3,2,1,0:T(8,128)(2,1)S(1)} %pack.5.refs_2_.refs_1_, f32[1152,128]{1,0:T(8,128)S(1)} %early.2.refs_3_.refs_2_, f32[1152,128]{1,0:T(8,128)S(1)} %collective-permute-done.16.refs_3_, ...), custom_call_target="tpu_custom_call" | custom-call | flops 30000001024 | bytes 4000000 | tf_op jit(solution)/shard_map/stage3/pallas_call | solution.py:406
  191.7 3.1 %collective-permute-done.21.refs_3_ = f32[1152,128]{1,0:T(8,128)S(1)} collective-permute-done((f32[1152,128]{1,0:T(8,128)S(1)}, f32[1152,128]{1,0:T(8,128)S(1)}, u32[]{:S(2)}, u32[]{:S(2)}) %collective-permute-start.21) | collective-permute-done | bytes 589856 | tf_op jit(solution)/shard_map/ppermute | solution.py:418
  194.7 5.2 %collective-permute-done.22.refs_4_ = f32[1152,128]{1,0:T(8,128)S(1)} collective-permute-done((f32[1152,128]{1,0:T(8,128)S(1)}, f32[1152,128]{1,0:T(8,128)S(1)}, u32[]{:S(2)}, u32[]{:S(2)}) %collective-permute-start.22) | collective-permute-done | bytes 589856 | tf_op jit(solution)/shard_map/ppermute | solution.py:418
  199.9 5.3 %stage3.3 = f32[1152,128]{1,0:T(8,128)S(1)} custom-call(s32[1]{0:T(128)} %bitcast.plane_ref, bf16[2,2,576,1024]{3,2,1,0:T(8,128)(2,1)S(1)} %bitcast.20, bf16[2,2,576,1152]{3,2,1,0:T(8,128)(2,1)S(1)} %pack.5.refs_2_.refs_1_, f32[1152,128]{1,0:T(8,128)S(1)} %early.3.refs_3_.refs_2_, f32[1152,128]{1,0:T(8,128)S(1)} %collective-permute-done.21.refs_3_, ...), custom_call_target="tpu_custom_call" | custom-call | flops 30000001024 | bytes 4000000 | tf_op jit(solution)/shard_map/stage3/pallas_call | solution.py:406
  (123 shorter events, 46.6 us)
Async XLA Ops:
  7.5 6.6 %collective-permute-start = (f32[18,288]{1,0:T(8,128)S(1)}, f32[18,288]{1,0:T(8,128)S(1)}, u32[]{:S(2)}, u32[]{:S(2)}) collective-permute-start(f32[18,288]{1,0:T(8,128)S(1)} %get-tuple-element.48), channel_id=1, source_target_pairs={{32,0},{33,1},{34,2},{35,3},{36,4},{37,5},{38,6},{39,7},{40,8},{41... | collective-permute-start | bytes 62216 | tf_op jit(solution)/shard_map/ppermute | solution.py:314
  11.0 12.6 %collective-permute-start.6 = (f32[18,1152]{1,0:T(8,128)S(1)}, f32[18,1152]{1,0:T(8,128)S(1)}, u32[]{:S(2)}, u32[]{:S(2)}) collective-permute-start(f32[18,1152]{1,0:T(8,128)S(1)} %slice.52), channel_id=1, source_target_pairs={{192,0},{193,1},{194,2},{195,3},{196,4},{197,5},{198,6},{199,7},{2... | collective-permute-start | bytes 248840 | tf_op jit(solution)/shard_map/ppermute | solution.py:300
  15.1 27.7 %all-to-all-start = ((f32[8,144,128]{2,1,0:T(8,128)}), f32[8,144,128]{2,1,0:T(8,128)S(1)}, u32[]{:S(2)}, u32[]{:S(2)}) async-start(f32[8,144,128]{2,1,0:T(8,128)} %broadcast_in_dim.8), calls=%async_computation | async-start | bytes 1179648 | tf_op jit(solution)/shard_map/all_to_all | solution.py:324
  23.3 104.4 %all-gather.2.cloned.1.call-start = ((), (), s32[]{:S(2)}) async-start(), calls=%async_computation.2 | async-start | bytes 5677056 | tf_op jit(solution)/shard_map/all_gather | solution.py:328
  42.7 47.9 %all-to-all-start.1 = ((f32[64,8,576]{2,1,0:T(8,128)}), f32[64,8,576]{2,1,0:T(8,128)S(1)}, u32[]{:S(2)}, u32[]{:S(2)}) async-start(f32[64,8,576]{2,1,0:T(8,128)} %convolution_bitcast_fusion), calls=%async_computation.1 | async-start | bytes 2621440 | tf_op jit(solution)/shard_map/all_to_all | solution.py:326
  48.4 24.6 %collective-permute-start.1 = (f32[1152,128]{1,0:T(8,128)S(1)}, f32[1152,128]{1,0:T(8,128)S(1)}, u32[]{:S(2)}, u32[]{:S(2)}) collective-permute-start(f32[1152,128]{1,0:T(8,128)S(1)} %bitcast.21), channel_id=1, source_target_pairs={{0,8},{8,16},{16,24},{24,0},{1,9},{9,17},{17,25},{25,1},{2,10},{10... | collective-permute-start | bytes 1769480 | tf_op jit(solution)/shard_map/ppermute | solution.py:333
  48.5 27.8 %collective-permute-start.3 = (f32[1152,128]{1,0:T(8,128)S(1)}, f32[1152,128]{1,0:T(8,128)S(1)}, u32[]{:S(2)}, u32[]{:S(2)}) collective-permute-start(f32[1152,128]{1,0:T(8,128)S(1)} %bitcast.22), channel_id=1, source_target_pairs={{0,24},{8,0},{16,8},{24,16},{1,25},{9,1},{17,9},{25,17},{2,26},{10... | collective-permute-start | bytes 1769480 | tf_op jit(solution)/shard_map/ppermute | solution.py:333
  73.8 12.7 %collective-permute-start.2 = (f32[576,128]{1,0:T(8,128)}, f32[576,128]{1,0:T(8,128)S(1)}, u32[]{:S(2)}, u32[]{:S(2)}) collective-permute-start(f32[576,128]{1,0:T(8,128)} %slice.60), channel_id=1, source_target_pairs={{0,8},{8,16},{16,24},{24,0},{1,9},{9,17},{17,25},{25,1},{2,10},{10... | collective-permute-start | bytes 884744 | tf_op jit(solution)/shard_map/ppermute | solution.py:336
  77.2 13.4 %collective-permute-start.4 = (f32[576,128]{1,0:T(8,128)}, f32[576,128]{1,0:T(8,128)}, u32[]{:S(2)}, u32[]{:S(2)}) collective-permute-start(f32[576,128]{1,0:T(8,128)} %slice.61), channel_id=1, source_target_pairs={{0,24},{8,0},{16,8},{24,16},{1,25},{9,1},{17,9},{25,17},{2,26},{10... | collective-permute-start | bytes 884744 | tf_op jit(solution)/shard_map/ppermute | solution.py:336
  100.5 8.0 %collective-permute-start.5 = (f32[576,1024]{1,0:T(8,128)S(1)}, f32[576,1024]{1,0:T(8,128)S(1)}, u32[]{:S(2)}, u32[]{:S(2)}) collective-permute-start(f32[576,1024]{1,0:T(8,128)S(1)} %invert.1.own_ref), channel_id=1, source_target_pairs={{0,32},{32,0},{1,33},{33,1},{2,34},{34,2},{3,35},{35,3},{4,36},{36... | collective-permute-start | bytes 7077896 | tf_op jit(solution)/shard_map/ppermute | solution.py:361
  110.0 17.6 %collective-permute-start.8 = (f32[1152,128]{1,0:T(8,128)S(1)}, f32[1152,128]{1,0:T(8,128)S(1)}, u32[]{:S(2)}, u32[]{:S(2)}) collective-permute-start(f32[1152,128]{1,0:T(8,128)S(1)} %stage0.2), channel_id=1, source_target_pairs={{0,192},{1,193},{2,194},{3,195},{4,196},{5,197},{6,198},{7,199},{8... | collective-permute-start | bytes 1769480 | tf_op jit(solution)/shard_map/ppermute | solution.py:418
  136.7 11.7 %collective-permute-start.10 = (f32[1152,128]{1,0:T(8,128)S(1)}, f32[1152,128]{1,0:T(8,128)S(1)}, u32[]{:S(2)}, u32[]{:S(2)}) collective-permute-start(f32[1152,128]{1,0:T(8,128)S(1)} %stage0.3), channel_id=1, source_target_pairs={{0,64},{1,65},{2,66},{3,67},{4,68},{5,69},{6,70},{7,71},{8,72},{9,... | collective-permute-start | bytes 1769480 | tf_op jit(solution)/shard_map/ppermute | solution.py:418
  137.4 18.1 %collective-permute-start.11 = (f32[1152,128]{1,0:T(8,128)S(1)}, f32[1152,128]{1,0:T(8,128)S(1)}, u32[]{:S(2)}, u32[]{:S(2)}) collective-permute-start(f32[1152,128]{1,0:T(8,128)S(1)} %stage0.3), channel_id=1, source_target_pairs={{0,192},{1,193},{2,194},{3,195},{4,196},{5,197},{6,198},{7,199},{8... | collective-permute-start | bytes 1769480 | tf_op jit(solution)/shard_map/ppermute | solution.py:418
  138.7 20.8 %collective-permute-start.13 = (f32[1152,128]{1,0:T(8,128)S(1)}, f32[1152,128]{1,0:T(8,128)S(1)}, u32[]{:S(2)}, u32[]{:S(2)}) collective-permute-start(f32[1152,128]{1,0:T(8,128)S(1)} %collective-permute-done.8.refs_4_), channel_id=1, source_target_pairs={{192,128},{193,129},{194,130},{195,131},{196,132},{197,133},{198,1... | collective-permute-start | bytes 1769480 | tf_op jit(solution)/shard_map/ppermute | solution.py:418
  140.0 22.8 %collective-permute-start.12 = (f32[576,1152]{1,0:T(8,128)}, f32[576,1152]{1,0:T(8,128)S(1)}, u32[]{:S(2)}, u32[]{:S(2)}) collective-permute-start(f32[576,1152]{1,0:T(8,128)} %copy-done.3), channel_id=1, source_target_pairs={{0,32},{32,0},{1,33},{33,1},{2,34},{34,2},{3,35},{35,3},{4,36},{36... | collective-permute-start | bytes 7962632 | tf_op jit(solution)/shard_map/ppermute | solution.py:379
  147.6 16.7 %collective-permute-start.14 = (f32[1152,128]{1,0:T(8,128)S(1)}, f32[1152,128]{1,0:T(8,128)S(1)}, u32[]{:S(2)}, u32[]{:S(2)}) collective-permute-start(f32[1152,128]{1,0:T(8,128)S(1)} %get-tuple-element.33), channel_id=1, source_target_pairs={{64,0},{65,1},{66,2},{67,3},{68,4},{69,5},{70,6},{71,7},{72,8},{73... | collective-permute-start | bytes 1769480 | tf_op jit(solution)/shard_map/ppermute | solution.py:418
  148.3 16.0 %collective-permute-start.15 = (f32[1152,128]{1,0:T(8,128)S(1)}, f32[1152,128]{1,0:T(8,128)S(1)}, u32[]{:S(2)}, u32[]{:S(2)}) collective-permute-start(f32[1152,128]{1,0:T(8,128)S(1)} %get-tuple-element.33), channel_id=1, source_target_pairs={{64,128},{65,129},{66,130},{67,131},{68,132},{69,133},{70,134},{71... | collective-permute-start | bytes 1769480 | tf_op jit(solution)/shard_map/ppermute | solution.py:418
  155.4 13.5 %collective-permute-start.18 = (f32[1152,128]{1,0:T(8,128)S(1)}, f32[1152,128]{1,0:T(8,128)S(1)}, u32[]{:S(2)}, u32[]{:S(2)}) collective-permute-start(f32[1152,128]{1,0:T(8,128)S(1)} %collective-permute-done.11.refs_4_), channel_id=1, source_target_pairs={{192,128},{193,129},{194,130},{195,131},{196,132},{197,133},{198,1... | collective-permute-start | bytes 1769480 | tf_op jit(solution)/shard_map/ppermute | solution.py:418
  159.5 9.4 %collective-permute-start.19 = (f32[1152,128]{1,0:T(8,128)S(1)}, f32[1152,128]{1,0:T(8,128)S(1)}, u32[]{:S(2)}, u32[]{:S(2)}) collective-permute-start(f32[1152,128]{1,0:T(8,128)S(1)} %get-tuple-element.37), channel_id=1, source_target_pairs={{64,0},{65,1},{66,2},{67,3},{68,4},{69,5},{70,6},{71,7},{72,8},{73... | collective-permute-start | bytes 1769480 | tf_op jit(solution)/shard_map/ppermute | solution.py:418
  162.8 6.1 %collective-permute-start.20 = (f32[1152,128]{1,0:T(8,128)S(1)}, f32[1152,128]{1,0:T(8,128)S(1)}, u32[]{:S(2)}, u32[]{:S(2)}) collective-permute-start(f32[1152,128]{1,0:T(8,128)S(1)} %get-tuple-element.37), channel_id=1, source_target_pairs={{64,128},{65,129},{66,130},{67,131},{68,132},{69,133},{70,134},{71... | collective-permute-start | bytes 1769480 | tf_op jit(solution)/shard_map/ppermute | solution.py:418
  164.4 17.0 %collective-permute-start.16 = (f32[1152,128]{1,0:T(8,128)S(1)}, f32[1152,128]{1,0:T(8,128)S(1)}, u32[]{:S(2)}, u32[]{:S(2)}) collective-permute-start(f32[1152,128]{1,0:T(8,128)S(1)} %stage2.2), channel_id=1, source_target_pairs={{0,192},{1,193},{2,194},{3,195},{4,196},{5,197},{6,198},{7,199},{8... | collective-permute-start | bytes 1769480 | tf_op jit(solution)/shard_map/ppermute | solution.py:418
  165.7 20.5 %collective-permute-start.17 = (f32[1152,128]{1,0:T(8,128)S(1)}, f32[1152,128]{1,0:T(8,128)S(1)}, u32[]{:S(2)}, u32[]{:S(2)}) collective-permute-start(f32[1152,128]{1,0:T(8,128)S(1)} %stage2.2), channel_id=1, source_target_pairs={{128,192},{129,193},{130,194},{131,195},{132,196},{133,197},{134,1... | collective-permute-start | bytes 1769480 | tf_op jit(solution)/shard_map/ppermute | solution.py:418
  169.0 25.7 %collective-permute-start.21 = (f32[1152,128]{1,0:T(8,128)S(1)}, f32[1152,128]{1,0:T(8,128)S(1)}, u32[]{:S(2)}, u32[]{:S(2)}) collective-permute-start(f32[1152,128]{1,0:T(8,128)S(1)} %stage2.3), channel_id=1, source_target_pairs={{0,192},{1,193},{2,194},{3,195},{4,196},{5,197},{6,198},{7,199},{8... | collective-permute-start | bytes 1769480 | tf_op jit(solution)/shard_map/ppermute | solution.py:418
  170.5 29.5 %collective-permute-start.22 = (f32[1152,128]{1,0:T(8,128)S(1)}, f32[1152,128]{1,0:T(8,128)S(1)}, u32[]{:S(2)}, u32[]{:S(2)}) collective-permute-start(f32[1152,128]{1,0:T(8,128)S(1)} %stage2.3), channel_id=1, source_target_pairs={{128,192},{129,193},{130,194},{131,195},{132,196},{133,197},{134,1... | collective-permute-start | bytes 1769480 | tf_op jit(solution)/shard_map/ppermute | solution.py:418
  (25 other events, 164.2 us)
Sparse Core Ops, SparseCore 0:
  26.7 92.4 all-gather.1
